TPU v7x, 512 devices: a whole 4x8x8 slice. The times are simulated.
512 devices in a mesh: cuts: 128 (over z, y, core), batch: 4 (over x).
Axes of the slice: x: 4, y: 8, z: 8, core: 2. Of those that a mesh axis runs over, the one named last changes fastest.
Arguments:
- blocks: bfloat16 [65536, 64, 128], P(('cuts', 'batch')), may hold values from -6 to 6
- environments: bfloat16 [65536, 64, 128], P(('cuts', 'batch')), may hold values from -0.5 to 0.5
- layers: bfloat16 [8, 64, 128], replicated, may hold values from -0.5 to 0.5
- selectors: bfloat16 [65536, 8, 128], P(('cuts', 'batch')), may hold values from -6 to 6
- classes: int32 [512, 128], P(('cuts', 'batch')), may hold values from 1 to 8
- routing: int32 [512, 128], P(('cuts', 'batch')), may hold values from 0 to 127, each once within a row
- left_edges: bfloat16 [64, 128], replicated, may hold values from -0.5 to 0.5
- right_edges: bfloat16 [64, 128], replicated, may hold values from -0.5 to 0.5
- owner_map: int32 [4096], replicated, may hold values from 0 to 4095, each once
Outputs:
- amplitudes: float32 [2, 4096], P(None, ('cuts', 'batch'))
Inputs may be any that keep to these rules, and one draw needn't show every extreme that they name: `routing`: each holder's row is a permutation of 0 to 127. `owner_map`: A permutation of the bitstrings.
All inputs are finite; a program needn't handle non-finite values.
Results may differ from a plain program's by a relative error of at most 0.009.
Values may be sent and summed in bfloat16 or wider, within the bound.
No kernel may reach another device: no remote copies, remote signals or barrier semaphores. Data moves between devices by JAX's collectives and lax.ppermute only.
A program may use at most 64 MiB of HBM per device.

v0:
```python
import functools

import jax
import jax.numpy as jnp
from jax import lax
from jax.sharding import Mesh
from jax.sharding import PartitionSpec as P

CUTS = ("cuts_0", "cuts_1", "cuts_2")
CUTS_BATCH = ("cuts_0", "cuts_1", "cuts_2", "batch")


def by_axis(shard, axes):
    return functools.reduce(lax.psum, axes, shard)


def block_form(matrix):
    half_count = matrix.shape[-1] // 2
    real_block = matrix[..., :half_count]
    imag_block = matrix[..., half_count:]
    upper_rows = jnp.concatenate([real_block, imag_block], axis=-1)
    lower_rows = jnp.concatenate([-imag_block, real_block], axis=-1)
    return jnp.concatenate([upper_rows, lower_rows], axis=-2)


def apply_phase(product, factors):
    half_count = product.shape[-1] // 2
    prod_real = product[..., :half_count]
    prod_imag = product[..., half_count:]
    fac_real = factors[..., :half_count].astype(jnp.float32)[:, None, :]
    fac_imag = factors[..., half_count:].astype(jnp.float32)[:, None, :]
    out_real = prod_real * fac_real - prod_imag * fac_imag
    out_imag = prod_real * fac_imag + prod_imag * fac_real
    return jnp.concatenate([out_real, out_imag], axis=-1)


def advance(blocks_now, factors, levels, tables):
    slot_count = blocks_now.shape[0]
    block_rows = min(32, slot_count)
    ranking = jnp.argsort(-levels, stable=True)
    blocks_now = blocks_now[ranking]
    factors = factors[ranking]
    levels = levels[ranking]
    for layer_index in range(tables.shape[0]):
        active = jnp.sum((levels > layer_index).astype(jnp.int32))
        rounds = (active + block_rows - 1) // block_rows
        layer_factors = factors[:, layer_index, :]

        def apply(round_index, current, layer_index=layer_index, layer_factors=layer_factors):
            offset = round_index * block_rows
            portion = lax.dynamic_slice_in_dim(current, offset, block_rows, 0)
            portion_levels = lax.dynamic_slice_in_dim(levels, offset, block_rows, 0)
            portion_factors = lax.dynamic_slice_in_dim(layer_factors, offset, block_rows, 0)
            product = jnp.einsum(
                "sij,jk->sik", portion, tables[layer_index], preferred_element_type=jnp.float32
            )
            updated = apply_phase(product, portion_factors).astype(jnp.bfloat16)
            portion = jnp.where((portion_levels > layer_index)[:, None, None], updated, portion)
            return lax.dynamic_update_slice_in_dim(current, portion, offset, 0)

        blocks_now = lax.fori_loop(0, rounds, apply, blocks_now)
    return (blocks_now, ranking)


def contract(worked, partners):
    slot_count, bond_width, doubled = worked.shape
    parted = worked.reshape(slot_count, bond_width, 2, bond_width)
    products = jnp.einsum("sipj,sjk->pik", parted, partners, preferred_element_type=jnp.float32)
    real_part = products[0, :, :bond_width] - products[1, :, bond_width:]
    imag_part = products[0, :, bond_width:] + products[1, :, :bond_width]
    return (real_part, imag_part)


def amplitude_table(real_part, imag_part, left_edges, right_edges, owner_map):
    half_count = left_edges.shape[1] // 2
    left_real = left_edges[:, :half_count].astype(jnp.float32)
    left_imag = left_edges[:, half_count:].astype(jnp.float32)
    right_real = right_edges[:, :half_count].astype(jnp.float32)
    right_imag = right_edges[:, half_count:].astype(jnp.float32)
    wave_real = jnp.dot(real_part, right_real) - jnp.dot(imag_part, right_imag)
    wave_imag = jnp.dot(real_part, right_imag) + jnp.dot(imag_part, right_real)
    amp_real = jnp.dot(left_real.T, wave_real) - jnp.dot(left_imag.T, wave_imag)
    amp_imag = jnp.dot(left_real.T, wave_imag) + jnp.dot(left_imag.T, wave_real)
    flattened = jnp.stack([amp_real.reshape(-1), amp_imag.reshape(-1)])
    return flattened[:, owner_map]


def on_device(
    blocks, environments, layers, selectors, classes, routing, left_edges, right_edges, owner_map
):
    slot_count, bond_width, doubled = blocks.shape
    cut_count = lax.axis_size(CUTS)
    member = slot_count // cut_count
    tables = block_form(layers)
    levels = classes[0]
    sending = routing[0]
    worked, ranking = advance(blocks, selectors, levels, tables)
    inverse = jnp.argsort(ranking)
    worked = worked[inverse[sending]]
    partners = lax.all_to_all(
        environments.reshape(cut_count, member, bond_width, doubled),
        CUTS,
        split_axis=0,
        concat_axis=0,
        tiled=True,
    )
    partners = partners.reshape(slot_count, bond_width, doubled)
    real_part, imag_part = contract(worked, partners)
    holder_count = cut_count * lax.axis_size("batch")
    normalizer = (slot_count * holder_count) ** (-0.5)
    real_part, imag_part = (by_axis(real_part, CUTS_BATCH), by_axis(imag_part, CUTS_BATCH))
    amp_table = (
        amplitude_table(real_part, imag_part, left_edges, right_edges, owner_map) * normalizer
    )
    per_holder = amp_table.shape[1] // holder_count
    holder = lax.axis_index(CUTS) * lax.axis_size("batch") + lax.axis_index("batch")
    return lax.dynamic_slice_in_dim(amp_table, holder * per_holder, per_holder, 1)


def solution(mesh):
    torus = Mesh(
        mesh.devices.reshape(8, 8, 2, mesh.shape["batch"]), ("cuts_0", "cuts_1", "cuts_2", "batch")
    )
    in_specs = (
        P(CUTS_BATCH, None, None),
        P(CUTS_BATCH, None, None),
        P(),
        P(CUTS_BATCH, None, None),
        P(CUTS_BATCH, None),
        P(CUTS_BATCH, None),
        P(),
        P(),
        P(),
    )
    out_specs = P(None, CUTS_BATCH)
    return jax.shard_map(
        on_device, mesh=torus, in_specs=in_specs, out_specs=out_specs, check_vma=False
    )
```

profile of v0, /device:TPU:1, one launch (start us, length us, event | category | flops | bytes accessed | tf_op | source)
XLA Modules:
  0.0 275.4 jit_solution(3500946976895617982)
XLA Ops:
  0.0 19.0 %all-to-all-start = ((bf16[128,1,64,128]{3,2,1,0:T(8,128)(2,1)}), bf16[128,1,64,128]{3,2,1,0:T(8,128)(2,1)}, u32[]{:S(2)}, u32[]{:S(2)}) async-start(bf16[128,1,64,128]{3,2,1,0:T(8,128)(2,1)} %bitcast.108), calls=%async_computation | async-start | bytes 4194304 | tf_op jit(solution)/shard_map/all_to_all | solution.py:100
  19.1 2.5 sort.34
  30.5 2.1 gather_fusion
  32.7 17.2 %while.80 = (s32[]{:T(128)}, bf16[128,64,128]{2,1,0:T(8,128)(2,1)}, s32[]{:T(128)}, s32[128]{0:T(128)S(1)}, bf16[8,128,128]{2,1,0:T(8,128)(2,1)S(1)}, /*index=5*...) while((s32[]{:T(128)}, bf16[128,64,128]{2,1,0:T(8,128)(2,1)}, ...), condition=%wide.region_3.4_spmd, body=%wide.region_2.3_spmd.sunk | while | flops 69472296 | bytes 4792699 | solution.py:61
  34.8 2.3 fusion.127
  39.1 2.3 fusion.127
  43.4 2.3 fusion.127
  47.7 2.3 fusion.127
  49.9 17.2 %while.81 = (s32[]{:T(128)}, bf16[128,64,128]{2,1,0:T(8,128)(2,1)}, s32[]{:T(128)}, s32[128]{0:T(128)S(1)}, bf16[8,128,128]{2,1,0:T(8,128)(2,1)S(1)}, /*index=5*...) while((s32[]{:T(128)}, bf16[128,64,128]{2,1,0:T(8,128)(2,1)}, ...), condition=%wide.region_6.7_spmd, body=%wide.region_5.6_spmd.sunk | while | flops 69472296 | bytes 4792699 | solution.py:61
  52.0 2.3 fusion.131
  56.3 2.3 fusion.131
  60.6 2.3 fusion.131
  64.9 2.3 fusion.131
  68.0 17.2 %while.82 = (s32[]{:T(128)}, bf16[128,64,128]{2,1,0:T(8,128)(2,1)}, s32[]{:T(128)}, s32[128]{0:T(128)S(1)}, bf16[8,128,128]{2,1,0:T(8,128)(2,1)S(1)}, /*index=5*...) while((s32[]{:T(128)}, bf16[128,64,128]{2,1,0:T(8,128)(2,1)}, ...), condition=%wide.region_9.10_spmd, body=%wide.region_8.9_spmd.sunk | while | flops 69472296 | bytes 4792699 | solution.py:61
  70.1 2.3 fusion.135
  74.4 2.3 fusion.135
  78.7 2.3 fusion.135
  82.9 2.3 fusion.135
  85.2 17.2 %while.83 = (s32[]{:T(128)}, bf16[128,64,128]{2,1,0:T(8,128)(2,1)}, s32[]{:T(128)}, s32[128]{0:T(128)S(1)}, bf16[8,128,128]{2,1,0:T(8,128)(2,1)S(1)}, /*index=5*...) while((s32[]{:T(128)}, bf16[128,64,128]{2,1,0:T(8,128)(2,1)}, ...), condition=%wide.region_12.13_spmd, body=%wide.region_11.12_spmd.sunk | while | flops 69472296 | bytes 4792699 | solution.py:61
  87.2 2.3 fusion.139
  91.5 2.3 fusion.139
  95.8 2.3 fusion.139
  100.1 2.3 fusion.139
  103.3 17.2 %while.84 = (s32[]{:T(128)}, bf16[128,64,128]{2,1,0:T(8,128)(2,1)}, s32[]{:T(128)}, s32[128]{0:T(128)S(1)}, bf16[8,128,128]{2,1,0:T(8,128)(2,1)S(1)}, /*index=5*...) while((s32[]{:T(128)}, bf16[128,64,128]{2,1,0:T(8,128)(2,1)}, ...), condition=%wide.region_15.16_spmd, body=%wide.region_14.15_spmd.sunk | while | flops 69472296 | bytes 4792699 | solution.py:61
  105.3 2.3 fusion.143
  109.6 2.3 fusion.143
  113.9 2.3 fusion.143
  118.2 2.3 fusion.143
  120.5 17.2 %while.85 = (s32[]{:T(128)}, bf16[128,64,128]{2,1,0:T(8,128)(2,1)}, s32[]{:T(128)}, s32[128]{0:T(128)S(1)}, bf16[8,128,128]{2,1,0:T(8,128)(2,1)S(1)}, /*index=5*...) while((s32[]{:T(128)}, bf16[128,64,128]{2,1,0:T(8,128)(2,1)}, ...), condition=%wide.region_18.19_spmd, body=%wide.region_17.18_spmd.sunk | while | flops 69472296 | bytes 4792699 | solution.py:61
  122.5 2.3 fusion.147
  126.8 2.3 fusion.147
  131.1 2.3 fusion.147
  135.4 2.3 fusion.147
  138.5 13.1 %while.86 = (s32[]{:T(128)}, bf16[128,64,128]{2,1,0:T(8,128)(2,1)}, s32[]{:T(128)}, s32[128]{0:T(128)S(1)}, bf16[8,128,128]{2,1,0:T(8,128)(2,1)S(1)}, /*index=5*...) while((s32[]{:T(128)}, bf16[128,64,128]{2,1,0:T(8,128)(2,1)}, ...), condition=%wide.region_21.22_spmd, body=%wide.region_20.21_spmd.sunk | while | flops 69472296 | bytes 4792699 | solution.py:61
  140.8 2.3 fusion.151
  145.1 2.3 fusion.151
  149.4 2.3 fusion.151
  151.6 2.5 sort.35
  155.5 4.3 %while.87 = (s32[]{:T(128)}, bf16[128,64,128]{2,1,0:T(8,128)(2,1)}, s32[]{:T(128)}, s32[128]{0:T(128)S(1)}, bf16[8,128,128]{2,1,0:T(8,128)(2,1)S(1)}, /*index=5*...) while((s32[]{:T(128)}, bf16[128,64,128]{2,1,0:T(8,128)(2,1)}, ...), condition=%wide.region_24.25_spmd, body=%wide.region_23.24_spmd.sunk | while | flops 69472296 | bytes 4792699 | solution.py:61
  157.5 2.3 fusion.155
  159.8 3.7 %gather_fusion.4 = bf16[128,64,128]{2,1,0:T(8,128)(2,1)} fusion(bf16[128,64,128]{2,1,0:T(8,128)(2,1)} %get-tuple-element.279, s32[1024]{0:T(1024)S(1)} %pad_clamp_fusion), kind=kCustom, calls=%fused_computation.4 | custom fusion | bytes 4194816 | tf_op jit(solution)/shard_map/gather | solution.py:99
  163.5 4.6 %copy.36 = bf16[128,64,128]{0,1,2:T(8,128)(2,1)} copy(bf16[128,64,128]{2,1,0:T(8,128)(2,1)} %gather_fusion.4) | data formatting | bytes 4194304 | tf_op jit(solution)/shard_map/reshape | solution.py:67
  168.1 3.7 %fusion.51 = f32[2,64,128]{2,1,0:T(8,128)S(1)} fusion(bf16[128,64,2,64]{0,1,3,2:T(8,128)(2,1)} %bitcast.109, bf16[128,1,64,128]{3,2,1,0:T(8,128)(2,1)} %all-to-all-done), kind=kOutput, calls=%fused_computation.105 | convolution fusion | flops 268435456 | bytes 4259840 | tf_op jit(solution)/shard_map/sipj,sjk->pik/dot_general | solution.py:68
  171.9 27.8 %all-reduce.1 = (f32[64,64]{1,0:T(8,128)S(1)}, f32[64,64]{1,0:T(8,128)S(1)}) all-reduce(f32[64,64]{1,0:T(8,128)S(1)} %get-tuple-element.436, f32[64,64]{1,0:T(8,128)S(1)} %get-tuple-element.435), channel_id=1, replica_groups=mesh['cuts_0'=8,'cuts_1'=8,'cuts_2'=2,'batch'=4] {'cuts_0'}, use_global_device_ids=true, to_apply=%region_26.27 | all-reduce | flops 8192 | bytes 65536 | tf_op jit(solution)/shard_map/psum | solution.py:14
  199.7 23.1 %all-reduce = (f32[64,64]{1,0:T(8,128)S(1)}, f32[64,64]{1,0:T(8,128)S(1)}) all-reduce(f32[64,64]{1,0:T(8,128)S(1)} %get-tuple-element.387, f32[64,64]{1,0:T(8,128)S(1)} %get-tuple-element.388), channel_id=1, replica_groups=mesh['cuts_0'=8,'cuts_1'=8,'cuts_2'=2,'batch'=4] {'cuts_1'}, use_global_device_ids=true, to_apply=%region_27.28 | all-reduce | flops 8192 | bytes 65536 | tf_op jit(solution)/shard_map/psum | solution.py:14
  222.8 17.7 %all-reduce.3 = (f32[64,64]{1,0:T(8,128)S(1)}, f32[64,64]{1,0:T(8,128)S(1)}) all-reduce(f32[64,64]{1,0:T(8,128)S(1)} %get-tuple-element.385, f32[64,64]{1,0:T(8,128)S(1)} %get-tuple-element.386), channel_id=1, replica_groups=mesh['cuts_0'=8,'cuts_1'=8,'cuts_2'=2,'batch'=4] {'cuts_2'}, use_global_device_ids=true, to_apply=%region_28.29 | all-reduce | flops 8192 | bytes 65536 | tf_op jit(solution)/shard_map/psum | solution.py:14
  240.6 14.0 %all-reduce.2 = (bf16[64,64]{1,0:T(8,128)(2,1)S(1)}, bf16[64,64]{1,0:T(8,128)(2,1)S(1)}) all-reduce(f32[64,64]{1,0:T(8,128)S(1)} %get-tuple-element.391, f32[64,64]{1,0:T(8,128)S(1)} %get-tuple-element.392), channel_id=1, replica_groups=mesh['cuts_0'=8,'cuts_1'=8,'cuts_2'=2,'batch'=4] {'batch'}, use_global_device_ids=true, to_apply=%region_29.30 | all-reduce | flops 8192 | bytes 49152 | tf_op jit(solution)/shard_map/psum | solution.py:14
  258.4 15.7 %gather_fusion.5 = f32[4096,2]{1,0:T(8,128)} fusion(f32[2,4096]{0,1:T(8,128)} %copy.33, s32[4096]{0:T(1024)S(1)} %fusion.58), kind=kCustom, calls=%fused_computation.5 | custom fusion | bytes 81920 | tf_op jit(solution)/shard_map/gather | solution.py:85
  (167 shorter events, 69.6 us)
Async XLA Ops:
  0.0 30.5 %copy-start = (bf16[128,64,128]{2,1,0:T(8,128)(2,1)S(1)}, bf16[128,64,128]{2,1,0:T(8,128)(2,1)}, u32[]{:S(2)}) copy-start(bf16[128,64,128]{2,1,0:T(8,128)(2,1)} %param.25) | copy-start | bytes 6291460
  0.0 19.0 %copy-start.1 = (s32[1,128]{1,0:T(1,128)S(1)}, s32[1,128]{1,0:T(1,128)}, u32[]{:S(2)}) copy-start(s32[1,128]{1,0:T(1,128)} %param.29) | copy-start | bytes 1540
  0.0 28.5 %copy-start.3 = (bf16[128,8,128]{2,1,0:T(8,128)(2,1)S(1)}, bf16[128,8,128]{2,1,0:T(8,128)(2,1)}, u32[]{:S(2)}) copy-start(bf16[128,8,128]{2,1,0:T(8,128)(2,1)} %param.28) | copy-start | bytes 786436
  0.0 168.1 %all-to-all-start = ((bf16[128,1,64,128]{3,2,1,0:T(8,128)(2,1)}), bf16[128,1,64,128]{3,2,1,0:T(8,128)(2,1)}, u32[]{:S(2)}, u32[]{:S(2)}) async-start(bf16[128,1,64,128]{3,2,1,0:T(8,128)(2,1)} %bitcast.108), calls=%async_computation | async-start | bytes 4194304 | tf_op jit(solution)/shard_map/all_to_all | solution.py:100
  19.1 11.3 %copy-start.2 = (bf16[8,64,128]{2,1,0:T(8,128)(2,1)S(1)}, bf16[8,64,128]{2,1,0:T(8,128)(2,1)}, u32[]{:S(2)}) copy-start(bf16[8,64,128]{2,1,0:T(8,128)(2,1)} %param.27) | copy-start | bytes 393220
  138.5 15.6 %copy-start.7 = (s32[1,128]{1,0:T(1,128)S(1)}, s32[1,128]{1,0:T(1,128)}, u32[]{:S(2)}) copy-start(s32[1,128]{1,0:T(1,128)} %param.30) | copy-start | bytes 1540
  163.5 4.6 %copy-start.6 = (s32[4096]{0:T(1024)S(1)}, s32[4096]{0:T(1024)}, u32[]{:S(2)}) copy-start(s32[4096]{0:T(1024)} %param.33) | copy-start | bytes 49156
  168.1 86.4 %copy-start.4 = (bf16[64,128]{1,0:T(8,128)(2,1)S(1)}, bf16[64,128]{1,0:T(8,128)(2,1)}, u32[]{:S(2)}) copy-start(bf16[64,128]{1,0:T(8,128)(2,1)} %param.32) | copy-start | bytes 49156
  168.1 87.1 %copy-start.5 = (bf16[64,128]{1,0:T(8,128)(2,1)S(1)}, bf16[64,128]{1,0:T(8,128)(2,1)}, u32[]{:S(2)}) copy-start(bf16[64,128]{1,0:T(8,128)(2,1)} %param.31) | copy-start | bytes 49156
where the time goes:
time: 280 us; the launch traced here: 275 us
  other arithmetic  90 us (32%)
  blocking collectives  82.6 us (30%)
  matrix products  42 us (15%)
  local copies, waits for them, and re-layouts  36 us (13%)
  starting transfers between devices  19 us (7%)
  between operations  5.18 us (2%)
    psum x4, blocking collectives, by_axis(): return functools.reduce(lax.psum, axes, shard)  82.6 us
    dynamic_update_slice x28, other arithmetic, apply(): return lax.dynamic_update_slice_in_dim(current, portion, offset, 0)  63.5 us
    dot_general x28, matrix products, apply(): jnp.einsum('sij,jk->sik', portion, tables[layer_index], preferred_element...  36.8 us
    all_to_all x1, starting transfers between devices, on_device(): lax.all_to_all(environments.reshape(cut_count, member, bond_width, double...  19 us
    gather x1, local copies, waits for them, and re-layouts, amplitude_table(): return flattened[:, owner_map]  15.7 us
    another operation x28, other arithmetic  14.9 us
  transfers between devices with their start and end apart: 1, of which 0 were waited for; matrix products, arithmetic and copies ran while one was open for 52% of the time, Pallas kernels for 0%

commit v1 on v0

v1 whole, which is shorter than its diff:
```python
import jax
import jax.numpy as jnp
from jax import lax
from jax.experimental import pallas as pl
from jax.experimental.pallas import tpu as pltpu
from jax.sharding import Mesh
from jax.sharding import PartitionSpec as P

CUTS = ("cuts_0", "cuts_1", "cuts_2")
CUTS_BATCH = ("cuts_0", "cuts_1", "cuts_2", "batch")
PLANE = ("cuts_0", "cuts_1")
NEAR = ("cuts_2", "batch")
TOGETHER = 8


def lower_half(shape):
    return lax.broadcasted_iota(jnp.int32, shape, len(shape) - 1) < shape[-1] // 2


def times_i(matrix):
    turned = pltpu.roll(matrix, matrix.shape[-1] // 2, axis=matrix.ndim - 1)
    return jnp.where(lower_half(matrix.shape), -turned, turned)


def advance_kernel(
    levels, sending, blocks, selectors, layers, left, right, owners, packed, left_cols, right_cols, tables
):
    depth, bond, doubled = layers.shape
    slots = blocks.shape[0]
    for layer in range(depth):
        plain = layers[layer].astype(jnp.float32)
        turned = times_i(plain)
        tables[layer, :bond, :doubled] = plain.astype(jnp.bfloat16)
        tables[layer, :bond, doubled:] = turned.astype(jnp.bfloat16)
        tables[layer, bond:, :doubled] = turned.astype(jnp.bfloat16)
        tables[layer, bond:, doubled:] = (-plain).astype(jnp.bfloat16)

    def stacked(edges):
        return jnp.concatenate([edges[:, :bond], edges[:, bond:]], axis=0)

    left_rows = stacked(left[...])
    right_rows = stacked(right[...])
    width = 512

    def columns(step, carry):
        at = pl.ds(pl.multiple_of(step * width, width), width)
        owner = owners[:, at]
        codes = lax.broadcasted_iota(jnp.int32, (bond, width), 0)
        by_left = jnp.where(codes == owner // bond, 1.0, 0.0).astype(jnp.bfloat16)
        by_right = jnp.where(codes == owner % bond, 1.0, 0.0).astype(jnp.bfloat16)
        left_cols[:, at] = jnp.dot(left_rows, by_left, preferred_element_type=jnp.float32).astype(jnp.bfloat16)
        right_cols[:, at] = jnp.dot(right_rows, by_right, preferred_element_type=jnp.float32)
        return carry

    lax.fori_loop(0, owners.shape[1] // width, columns, 0)

    def group(index, carry):
        first = index * TOGETHER
        slot = [sending[0, first + k] for k in range(TOGETHER)]
        level = [levels[0, slot[k]] for k in range(TOGETHER)]
        current = [blocks[slot[k]] for k in range(TOGETHER)]
        straight, crossed = [], []
        for k in range(TOGETHER):
            factor = selectors[slot[k]].astype(jnp.float32)
            swapped = pltpu.roll(factor, bond, axis=1)
            mask = lower_half(factor.shape)
            straight.append(jnp.where(mask, factor, swapped))
            crossed.append(jnp.where(mask, swapped, factor))
        for layer in range(depth):
            product = jnp.dot(
                jnp.concatenate(current, axis=0), tables[layer], preferred_element_type=jnp.float32
            )
            for k in range(TOGETHER):
                rows = product[k * bond : (k + 1) * bond]
                updated = (
                    rows[:, :doubled] * straight[k][layer : layer + 1]
                    + rows[:, doubled:] * crossed[k][layer : layer + 1]
                )
                current[k] = lax.select(level[k] > layer, updated.astype(jnp.bfloat16), current[k])
        mask = lower_half((bond, doubled))
        for k in range(0, TOGETHER, 2):
            one = current[k].astype(jnp.float32)
            two = current[k + 1].astype(jnp.float32)
            real = jnp.where(mask, one, pltpu.roll(two, bond, axis=1)).astype(jnp.bfloat16)
            imag = jnp.where(mask, pltpu.roll(one, bond, axis=1), two).astype(jnp.bfloat16)
            quad, part = divmod(k, 4)
            lanes = slice(part * bond, part * bond + doubled)
            packed[index * (TOGETHER // 4) + quad, :bond, lanes] = real
            packed[index * (TOGETHER // 4) + quad, bond:, lanes] = imag
        return carry

    lax.fori_loop(0, slots // TOGETHER, group, 0)


def amplitude_kernel(packed, partners, left_cols, right_cols, partial, real_rows, imag_rows, *, scale):
    quads, doubled, depth = packed.shape
    bond = doubled // 2
    total = jnp.zeros((doubled, doubled), jnp.float32)
    for quad in range(quads):
        total = total + jnp.dot(packed[quad], partners[quad], preferred_element_type=jnp.float32)
    core = (total[:bond] + times_i(total[bond:])) * scale
    whole = jnp.concatenate([core, times_i(core)], axis=0)
    high = whole.astype(jnp.bfloat16)
    low = (whole - high.astype(jnp.float32)).astype(jnp.bfloat16)
    pieces = jnp.concatenate([high.astype(jnp.float32), low.astype(jnp.float32)], axis=0).T.astype(jnp.bfloat16)
    width = 512
    for start in range(0, left_cols.shape[1], width):
        cols = left_cols[:, start : start + width]
        half = jnp.dot(pieces, jnp.concatenate([cols, cols], axis=0), preferred_element_type=jnp.float32)
        half_real, half_imag = half[:bond], half[bond:]
        right_real = right_cols[:bond, start : start + width]
        right_imag = right_cols[bond:, start : start + width]
        real = jnp.sum(half_real * right_real - half_imag * right_imag, axis=0, keepdims=True)
        imag = jnp.sum(half_real * right_imag + half_imag * right_real, axis=0, keepdims=True)
        for tile in range(width // 128):
            row = start // 128 + tile
            real_rows[row : row + 1, :] = real[:, tile * 128 : (tile + 1) * 128]
            imag_rows[row : row + 1, :] = imag[:, tile * 128 : (tile + 1) * 128]
    real, imag = real_rows[...], imag_rows[...]
    first = lax.broadcasted_iota(jnp.int32, real.shape, 1) % 16 < 8
    half_rows = real.shape[0]
    partial[:half_rows] = jnp.where(first, real, pltpu.roll(imag, 8, axis=1))
    partial[half_rows:] = jnp.where(first, pltpu.roll(real, 120, axis=1), imag)


def fold_kernel(arrived, summed):
    summed[...] = jnp.broadcast_to(jnp.sum(arrived[...], axis=0, keepdims=True), summed.shape)


def finish_kernel(place, arrived, out):
    total = jnp.broadcast_to(jnp.sum(arrived[...], axis=0, keepdims=True), (8, 128))
    total = pltpu.roll(total, (128 - 16 * place[0]) % 128, axis=1)
    out[0:1, :] = total[0:1, 0:8]
    out[1:2, :] = total[0:1, 8:16]


VMEM = pl.BlockSpec(memory_space=pltpu.VMEM)
SMEM = pl.BlockSpec(memory_space=pltpu.SMEM)


def on_device(
    blocks, environments, layers, selectors, classes, routing, left_edges, right_edges, owner_map
):
    slots, bond, doubled = blocks.shape
    depth = layers.shape[0]
    bits = owner_map.shape[0]
    near = lax.axis_size(NEAR)
    plane = lax.axis_size(PLANE)
    partners = lax.all_to_all(environments, CUTS, split_axis=0, concat_axis=0, tiled=True)
    per = bits // (near * plane)
    owners = owner_map.reshape(2, plane // 2, near, per).transpose(1, 2, 0, 3).reshape(1, bits)
    packed, left_cols, right_cols = pl.pallas_call(
        advance_kernel,
        out_shape=(
            jax.ShapeDtypeStruct((slots // 4, doubled, 4 * bond), jnp.bfloat16),
            jax.ShapeDtypeStruct((doubled, bits), jnp.bfloat16),
            jax.ShapeDtypeStruct((doubled, bits), jnp.float32),
        ),
        in_specs=[SMEM, SMEM] + [VMEM] * 6,
        out_specs=(VMEM,) * 3,
        scratch_shapes=[pltpu.VMEM((depth, doubled, 2 * doubled), jnp.bfloat16)],
        compiler_params=pltpu.CompilerParams(vmem_limit_bytes=16 << 20),
        name="advance",
    )(classes, routing, blocks, selectors, layers, left_edges, right_edges, owners)
    rows = bits * 2 // doubled
    scale = float(slots * near * plane) ** -0.5
    partial = pl.pallas_call(
        lambda *refs: amplitude_kernel(*refs, scale=scale),
        out_shape=jax.ShapeDtypeStruct((rows, doubled), jnp.float32),
        in_specs=[VMEM] * 4,
        out_specs=VMEM,
        scratch_shapes=[pltpu.VMEM((rows // 2, doubled), jnp.float32)] * 2,
        compiler_params=pltpu.CompilerParams(vmem_limit_bytes=16 << 20),
        name="amplitudes",
    )(packed, partners.reshape(slots // 4, 4 * bond, doubled), left_cols, right_cols)
    arrived = lax.all_to_all(partial, PLANE, split_axis=0, concat_axis=0, tiled=True)
    summed = pl.pallas_call(
        fold_kernel,
        out_shape=jax.ShapeDtypeStruct((near, doubled), jnp.float32),
        in_specs=[VMEM],
        out_specs=VMEM,
        name="fold",
    )(arrived)
    arrived = lax.all_to_all(summed, NEAR, split_axis=0, concat_axis=0, tiled=True)
    place = lax.axis_index(NEAR).reshape(1).astype(jnp.int32)
    return pl.pallas_call(
        finish_kernel,
        out_shape=jax.ShapeDtypeStruct((2, per), jnp.float32),
        in_specs=[SMEM, VMEM],
        out_specs=VMEM,
        name="finish",
    )(place, arrived)


def solution(mesh):
    torus = Mesh(
        mesh.devices.reshape(8, 8, 2, mesh.shape["batch"]), ("cuts_0", "cuts_1", "cuts_2", "batch")
    )
    in_specs = (
        P(CUTS_BATCH, None, None),
        P(CUTS_BATCH, None, None),
        P(),
        P(CUTS_BATCH, None, None),
        P(CUTS_BATCH, None),
        P(CUTS_BATCH, None),
        P(),
        P(),
        P(),
    )
    out_specs = P(None, CUTS_BATCH)
    return jax.shard_map(
        on_device, mesh=torus, in_specs=in_specs, out_specs=out_specs, check_vma=False
    )
```

time: 280 us -> 108 us (0.39); the launches traced: 275 us -> 107 us
  other arithmetic: 90 us -> 0 us
  blocking collectives: 82.6 us -> 18.5 us
  matrix products: 42 us -> 0 us
  waiting for transfers between devices: 0.01 us -> 26.5 us
  Pallas kernels: 0 us -> 25.9 us
  local copies, waits for them, and re-layouts: 36 us -> 11.5 us
  starting transfers between devices: 19 us -> 24.9 us
  between operations: 5.18 us -> 0.09 us
    psum x4 -> x0, blocking collectives: 82.6 us -> none  [by_axis(): return functools.reduce(lax.psum, axes, shard)]
    dynamic_update_slice x28 -> x0, other arithmetic: 63.5 us -> none  [apply(): return lax.dynamic_update_slice_in_dim(current, portion, offset, 0)]
    dot_general x37 -> x0, matrix products: 42 us -> none  [the longest x28 36.8 us: apply(): jnp.einsum('sij,jk->sik', portion, tables[layer_index], preferred_element...]
    all_to_all x1 -> x2, waiting for transfers between devices: 0.01 us -> 26.5 us  [the longest x1 21.9 us: on_device(): lax.all_to_all(environments, CUTS, split_axis=0, concat_axis=0, tiled=True)]
    pallas_call x0 -> x4, Pallas kernels: none -> 25.9 us  [the longest x1 21.5 us: on_device(): pl.pallas_call(advance_kernel, out_shape=(jax.ShapeDtypeStruct((slots //...]
    gather x6 -> x0, local copies, waits for them, and re-layouts: 24.7 us -> none  [the longest x1 15.7 us: amplitude_table(): return flattened[:, owner_map]]
    all_to_all x0 -> x1, blocking collectives: none -> 18.5 us  [on_device(): lax.all_to_all(partial, PLANE, split_axis=0, concat_axis=0, tiled=True)]
    another operation x29 -> x0, other arithmetic: 15 us -> none
  transfers between devices with their start and end apart: 1 -> 2, of which waited for: 0 -> 2; matrix products, arithmetic and copies ran while one was open for 52% -> 1% of each run, Pallas kernels for 0% -> 20%
where the time goes in v1:
time: 108 us; the launch traced here: 107 us
  waiting for transfers between devices  26.5 us (25%)
  Pallas kernels  25.9 us (24%)
  starting transfers between devices  24.9 us (23%)
  blocking collectives  18.5 us (17%)
  local copies, waits for them, and re-layouts  11.5 us (11%)
    all_to_all x1, waiting for transfers between devices, on_device(): lax.all_to_all(environments, CUTS, split_axis=0, concat_axis=0, tiled=True)  21.9 us
    pallas_call x1, Pallas kernels, on_device(): pl.pallas_call(advance_kernel, out_shape=(jax.ShapeDtypeStruct((slots //...  21.5 us
    all_to_all x1, starting transfers between devices, on_device(): lax.all_to_all(environments, CUTS, split_axis=0, concat_axis=0, tiled=True)  18.6 us
    all_to_all x1, blocking collectives, on_device(): lax.all_to_all(partial, PLANE, split_axis=0, concat_axis=0, tiled=True)  18.5 us
    unnamed x26, local copies, waits for them, and re-layouts  10.8 us
    all_to_all x1, starting transfers between devices, on_device(): lax.all_to_all(summed, NEAR, split_axis=0, concat_axis=0, tiled=True)  6.33 us
    all_to_all x1, waiting for transfers between devices, on_device(): lax.all_to_all(summed, NEAR, split_axis=0, concat_axis=0, tiled=True)  4.56 us
  transfers between devices with their start and end apart: 2, of which 2 were waited for; matrix products, arithmetic and copies ran while one was open for 1% of the time, Pallas kernels for 20%

profile of v1, /device:TPU:1, one launch (start us, length us, event | category | flops | bytes accessed | tf_op | source)
XLA Modules:
  0.0 107.3 jit_solution(3457157129474714164)
XLA Ops:
  0.0 0.0 copy-start.11
  0.0 0.0 copy-start.6
  0.0 0.0 copy-start.5
  0.0 18.6 %all-to-all-start = ((bf16[128,64,128]{2,1,0:T(8,128)(2,1)}), bf16[128,64,128]{2,1,0:T(8,128)(2,1)S(1)}, u32[]{:S(2)}, u32[]{:S(2)}) async-start(bf16[128,64,128]{2,1,0:T(8,128)(2,1)} %param.10), calls=%async_computation | async-start | bytes 4194304 | tf_op jit(solution)/shard_map/all_to_all | solution.py:149
  18.6 0.0 copy-done.11
  18.6 0.2 reshape.17
  18.8 0.2 copy.11
  19.0 0.4 reshape.18.owners
  19.3 0.0 copy-done.6
  19.4 0.0 copy-done.5
  19.4 0.0 copy-start.4
  19.4 1.6 %copy-done.4 = bf16[128,64,128]{2,1,0:T(8,128)(2,1)S(1)} copy-done((bf16[128,64,128]{2,1,0:T(8,128)(2,1)S(1)}, bf16[128,64,128]{2,1,0:T(8,128)(2,1)}, u32[]{:S(2)}) %copy-start.4) | copy-done | bytes 2097176
  21.0 0.0 copy-start.7
  21.0 0.7 copy-done.7
  21.7 0.0 copy-start.8
  21.7 0.7 copy-done.8
  22.4 0.0 copy-start.9
  22.4 0.7 copy-done.9
  23.1 0.0 copy-start.10
  23.1 0.7 copy-done.10
  23.7 21.5 %advance.1 = (bf16[32,128,256]{2,1,0:T(8,128)(2,1)S(1)}, bf16[128,4096]{1,0:T(8,128)(2,1)S(1)}, f32[128,4096]{1,0:T(8,128)S(1)}) custom-call(s32[1,128]{1,0:T(1,128)S(1)} %copy-done.9, s32[1,128]{1,0:T(1,128)S(1)} %copy-done.10, bf16[128,64,128]{2,1,0:T(8,128)(2,1)S(1)} %copy-done.4, bf16[128,8,128]{2,1,0:T(8,128)(2,1)S(1)} %copy-done.5, ...), custom_call_target="tpu_custom_call" | custom-call | tf_op jit(solution)/shard_map/advance/pallas_call | solution.py:152
  45.2 0.0 copy-start
  45.3 1.3 %copy-done = bf16[32,128,256]{2,1,0:T(8,128)(2,1)} copy-done((bf16[32,128,256]{2,1,0:T(8,128)(2,1)}, bf16[32,128,256]{2,1,0:T(8,128)(2,1)S(1)}, u32[]{:S(2)}) %copy-start) | copy-done | bytes 2097176
  46.6 0.0 copy-start.2
  46.6 1.3 %copy-done.2 = f32[128,4096]{1,0:T(8,128)} copy-done((f32[128,4096]{1,0:T(8,128)}, f32[128,4096]{1,0:T(8,128)S(1)}, u32[]{:S(2)}) %copy-start.2) | copy-done | bytes 2097176
  47.9 21.9 %all-to-all-done = bf16[128,64,128]{2,1,0:T(8,128)(2,1)S(1)} async-done(((bf16[128,64,128]{2,1,0:T(8,128)(2,1)}), bf16[128,64,128]{2,1,0:T(8,128)(2,1)S(1)}, u32[]{:S(2)}, u32[]{:S(2)}) %all-to-all-start) | async-done | bytes 2097184 | tf_op jit(solution)/shard_map/all_to_all | solution.py:149
  69.8 0.0 copy-start.1
  69.9 1.6 %copy-done.1 = bf16[32,128,256]{2,1,0:T(8,128)(2,1)S(1)} copy-done((bf16[32,128,256]{2,1,0:T(8,128)(2,1)S(1)}, bf16[32,128,256]{2,1,0:T(8,128)(2,1)}, u32[]{:S(2)}) %copy-start.1) | copy-done | bytes 2097176
  71.4 0.0 copy-start.3
  71.4 1.6 %copy-done.3 = f32[128,4096]{1,0:T(8,128)S(1)} copy-done((f32[128,4096]{1,0:T(8,128)S(1)}, f32[128,4096]{1,0:T(8,128)}, u32[]{:S(2)}) %copy-start.3) | copy-done | bytes 2097176
  73.0 1.6 %amplitudes.1 = f32[64,128]{1,0:T(8,128)S(1)} custom-call(bf16[32,128,256]{2,1,0:T(8,128)(2,1)S(1)} %copy-done.1, bf16[32,256,128]{2,1,0:T(8,128)(2,1)S(1)} %bitcast.11, bf16[128,4096]{1,0:T(8,128)(2,1)S(1)} %get-tuple-element.9.refs_2_, f32[128,4096]{1,0:T(8,128)S(1)} %copy-done.3), custom_call_target="tpu_custom_call" | custom-call | tf_op jit(solution)/shard_map/amplitudes/pallas_call | solution.py:167
  74.7 18.5 %all_to_all.27 = f32[64,1,128]{2,1,0:T(1,128)} all-to-all(f32[64,1,128]{2,1,0:T(1,128)S(1)} %bitcast.12), channel_id=1, replica_groups=mesh['cuts_0'=8,'cuts_1'=8,'cuts_2'=2,'batch'=4] {'cuts_0','cuts_1'}, dimensions={0} | all-to-all | bytes 65536 | tf_op jit(solution)/shard_map/all_to_all | solution.py:176
  93.1 1.4 %fold.1 = f32[8,128]{1,0:T(8,128)} custom-call(f32[64,128]{1,0:T(8,128)} %bitcast.14), custom_call_target="tpu_custom_call" | custom-call | tf_op jit(solution)/shard_map/fold/pallas_call | solution.py:177
  94.5 6.3 %all-to-all-start.2 = ((f32[8,1,128]{2,1,0:T(1,128)}), f32[8,1,128]{2,1,0:T(1,128)S(1)}, u32[]{:S(2)}, u32[]{:S(2)}) async-start(f32[8,1,128]{2,1,0:T(1,128)} %bitcast.15), calls=%async_computation.2 | async-start | bytes 8192 | tf_op jit(solution)/shard_map/all_to_all | solution.py:184
  100.8 4.6 %all-to-all-done.2 = f32[8,1,128]{2,1,0:T(1,128)S(1)} async-done(((f32[8,1,128]{2,1,0:T(1,128)}), f32[8,1,128]{2,1,0:T(1,128)S(1)}, u32[]{:S(2)}, u32[]{:S(2)}) %all-to-all-start.2) | async-done | bytes 4128 | tf_op jit(solution)/shard_map/all_to_all | solution.py:184
  105.4 0.0 copy-start.12
  105.4 0.6 copy-done.12
  106.0 1.4 %finish.1 = f32[2,8]{1,0:T(2,128)} custom-call(s32[1]{0:T(128)} %bitcast.place, f32[8,128]{1,0:T(8,128)} %bitcast.16), custom_call_target="tpu_custom_call" | custom-call | tf_op jit(solution)/shard_map/finish/pallas_call | solution.py:186
Async XLA Ops:
  0.0 18.6 %copy-start.11 = (s32[4096]{0:T(1024)S(1)}, s32[4096]{0:T(1024)}, u32[]{:S(2)}) copy-start(s32[4096]{0:T(1024)} %param.17) | copy-start | bytes 49156
  0.0 19.3 %copy-start.6 = (bf16[8,64,128]{2,1,0:T(8,128)(2,1)S(1)}, bf16[8,64,128]{2,1,0:T(8,128)(2,1)}, u32[]{:S(2)}) copy-start(bf16[8,64,128]{2,1,0:T(8,128)(2,1)} %layers.1) | copy-start | bytes 393220
  0.0 19.4 %copy-start.5 = (bf16[128,8,128]{2,1,0:T(8,128)(2,1)S(1)}, bf16[128,8,128]{2,1,0:T(8,128)(2,1)}, u32[]{:S(2)}) copy-start(bf16[128,8,128]{2,1,0:T(8,128)(2,1)} %selectors.1) | copy-start | bytes 786436
  0.0 69.8 %all-to-all-start = ((bf16[128,64,128]{2,1,0:T(8,128)(2,1)}), bf16[128,64,128]{2,1,0:T(8,128)(2,1)S(1)}, u32[]{:S(2)}, u32[]{:S(2)}) async-start(bf16[128,64,128]{2,1,0:T(8,128)(2,1)} %param.10), calls=%async_computation | async-start | bytes 4194304 | tf_op jit(solution)/shard_map/all_to_all | solution.py:149
  19.4 1.6 %copy-start.4 = (bf16[128,64,128]{2,1,0:T(8,128)(2,1)S(1)}, bf16[128,64,128]{2,1,0:T(8,128)(2,1)}, u32[]{:S(2)}) copy-start(bf16[128,64,128]{2,1,0:T(8,128)(2,1)} %blocks.1) | copy-start | bytes 6291460
  21.0 0.7 copy-start.7
  21.7 0.7 copy-start.8
  22.4 0.7 copy-start.9
  23.1 0.7 copy-start.10
  45.2 1.3 %copy-start = (bf16[32,128,256]{2,1,0:T(8,128)(2,1)}, bf16[32,128,256]{2,1,0:T(8,128)(2,1)S(1)}, u32[]{:S(2)}) copy-start(bf16[32,128,256]{2,1,0:T(8,128)(2,1)S(1)} %get-tuple-element.8.refs_0_) | copy-start | bytes 6291460
  46.6 1.3 %copy-start.2 = (f32[128,4096]{1,0:T(8,128)}, f32[128,4096]{1,0:T(8,128)S(1)}, u32[]{:S(2)}) copy-start(f32[128,4096]{1,0:T(8,128)S(1)} %get-tuple-element.10.refs_3_) | copy-start | bytes 6291460
  69.8 1.6 %copy-start.1 = (bf16[32,128,256]{2,1,0:T(8,128)(2,1)S(1)}, bf16[32,128,256]{2,1,0:T(8,128)(2,1)}, u32[]{:S(2)}) copy-start(bf16[32,128,256]{2,1,0:T(8,128)(2,1)} %copy-done) | copy-start | bytes 6291460
  71.4 1.6 %copy-start.3 = (f32[128,4096]{1,0:T(8,128)S(1)}, f32[128,4096]{1,0:T(8,128)}, u32[]{:S(2)}) copy-start(f32[128,4096]{1,0:T(8,128)} %copy-done.2) | copy-start | bytes 6291460
  94.5 10.9 %all-to-all-start.2 = ((f32[8,1,128]{2,1,0:T(1,128)}), f32[8,1,128]{2,1,0:T(1,128)S(1)}, u32[]{:S(2)}, u32[]{:S(2)}) async-start(f32[8,1,128]{2,1,0:T(1,128)} %bitcast.15), calls=%async_computation.2 | async-start | bytes 8192 | tf_op jit(solution)/shard_map/all_to_all | solution.py:184
  105.4 0.6 copy-start.12

commit v2 on v1

--- a/solution.py
+++ b/solution.py
@@ -23,10 +23,11 @@
 
 
 def advance_kernel(
-    levels, sending, blocks, selectors, layers, left, right, owners, packed, left_cols, right_cols, tables
+    core, levels, sending, blocks, selectors, layers, left, right, owners,
+    packed_other, packed_own, left_cols, right_cols, tables,
 ):
     depth, bond, doubled = layers.shape
-    slots = blocks.shape[0]
+    pairs = blocks.shape[0] // 2
     for layer in range(depth):
         plain = layers[layer].astype(jnp.float32)
         turned = times_i(plain)
@@ -49,14 +50,14 @@
         by_left = jnp.where(codes == owner // bond, 1.0, 0.0).astype(jnp.bfloat16)
         by_right = jnp.where(codes == owner % bond, 1.0, 0.0).astype(jnp.bfloat16)
         left_cols[:, at] = jnp.dot(left_rows, by_left, preferred_element_type=jnp.float32).astype(jnp.bfloat16)
-        right_cols[:, at] = jnp.dot(right_rows, by_right, preferred_element_type=jnp.float32)
+        right_cols[:, at] = jnp.dot(right_rows, by_right, preferred_element_type=jnp.float32).astype(jnp.bfloat16)
         return carry
 
     lax.fori_loop(0, owners.shape[1] // width, columns, 0)
 
-    def group(index, carry):
+    def group(index, carry, side, packed):
         first = index * TOGETHER
-        slot = [sending[0, first + k] for k in range(TOGETHER)]
+        slot = [sending[0, (first + k) * 2 + side] for k in range(TOGETHER)]
         level = [levels[0, slot[k]] for k in range(TOGETHER)]
         current = [blocks[slot[k]] for k in range(TOGETHER)]
         straight, crossed = [], []
@@ -89,27 +90,53 @@
             packed[index * (TOGETHER // 4) + quad, bond:, lanes] = imag
         return carry
 
-    lax.fori_loop(0, slots // TOGETHER, group, 0)
-
-
-def amplitude_kernel(packed, partners, left_cols, right_cols, partial, real_rows, imag_rows, *, scale):
-    quads, doubled, depth = packed.shape
+    steps = pairs // TOGETHER
+    lax.fori_loop(0, steps, lambda i, c: group(i, c, 1 - core[0], packed_other), 0)
+    lax.fori_loop(0, steps, lambda i, c: group(i, c, core[0], packed_own), 0)
+
+
+def amplitude_kernel(
+    core, own, other, partners_far, left_far, right_far, partial,
+    partners, left_cols, right_cols, real_rows, imag_rows, arrivals, *, scale,
+):
+    quads, doubled, depth = own.shape
     bond = doubled // 2
+    parts = 4
+    each = quads // parts
+
+    def load(part):
+        at = pl.ds(part * each * 4, each * 4)
+        return pltpu.make_async_copy(partners_far.at[at], partners.at[at], arrivals.at[part])
+
+    for part in range(parts):
+        load(part).start()
+    edges = (
+        pltpu.make_async_copy(left_far, left_cols, arrivals.at[parts]),
+        pltpu.make_async_copy(right_far, right_cols, arrivals.at[parts + 1]),
+    )
+    for edge in edges:
+        edge.start()
     total = jnp.zeros((doubled, doubled), jnp.float32)
-    for quad in range(quads):
-        total = total + jnp.dot(packed[quad], partners[quad], preferred_element_type=jnp.float32)
-    core = (total[:bond] + times_i(total[bond:])) * scale
-    whole = jnp.concatenate([core, times_i(core)], axis=0)
+    for part in range(parts):
+        load(part).wait()
+        for quad in range(part * each, (part + 1) * each):
+            for worked, side in ((own, core[0]), (other, 1 - core[0])):
+                rows = jnp.concatenate([partners[quad * 4 + k, side] for k in range(4)], axis=0)
+                total = total + jnp.dot(worked[quad], rows, preferred_element_type=jnp.float32)
+    core_matrix = (total[:bond] + times_i(total[bond:])) * scale
+    whole = jnp.concatenate([core_matrix, times_i(core_matrix)], axis=0)
     high = whole.astype(jnp.bfloat16)
     low = (whole - high.astype(jnp.float32)).astype(jnp.bfloat16)
     pieces = jnp.concatenate([high.astype(jnp.float32), low.astype(jnp.float32)], axis=0).T.astype(jnp.bfloat16)
     width = 512
+    for edge in edges:
+        edge.wait()
     for start in range(0, left_cols.shape[1], width):
         cols = left_cols[:, start : start + width]
         half = jnp.dot(pieces, jnp.concatenate([cols, cols], axis=0), preferred_element_type=jnp.float32)
         half_real, half_imag = half[:bond], half[bond:]
-        right_real = right_cols[:bond, start : start + width]
-        right_imag = right_cols[bond:, start : start + width]
+        right_real = right_cols[:bond, start : start + width].astype(jnp.float32)
+        right_imag = right_cols[bond:, start : start + width].astype(jnp.float32)
         real = jnp.sum(half_real * right_real - half_imag * right_imag, axis=0, keepdims=True)
         imag = jnp.sum(half_real * right_imag + half_imag * right_real, axis=0, keepdims=True)
         for tile in range(width // 128):
@@ -136,6 +163,7 @@
 
 VMEM = pl.BlockSpec(memory_space=pltpu.VMEM)
 SMEM = pl.BlockSpec(memory_space=pltpu.SMEM)
+FAR = pl.BlockSpec(memory_space=pltpu.HBM)
 
 
 def on_device(
@@ -146,33 +174,55 @@
     bits = owner_map.shape[0]
     near = lax.axis_size(NEAR)
     plane = lax.axis_size(PLANE)
-    partners = lax.all_to_all(environments, CUTS, split_axis=0, concat_axis=0, tiled=True)
+    cores = lax.axis_size("cuts_2")
+    partners = lax.all_to_all(
+        environments.reshape(plane, cores * bond, doubled), PLANE, split_axis=0, concat_axis=0, tiled=True
+    )
+    core = lax.axis_index("cuts_2").reshape(1).astype(jnp.int32)
+    place = lax.axis_index(NEAR).reshape(1).astype(jnp.int32)
     per = bits // (near * plane)
     owners = owner_map.reshape(2, plane // 2, near, per).transpose(1, 2, 0, 3).reshape(1, bits)
-    packed, left_cols, right_cols = pl.pallas_call(
+    core, place, owners = lax.optimization_barrier((core, place, owners))
+    packed_other, packed_own, left_cols, right_cols = pl.pallas_call(
         advance_kernel,
         out_shape=(
-            jax.ShapeDtypeStruct((slots // 4, doubled, 4 * bond), jnp.bfloat16),
+            jax.ShapeDtypeStruct((plane // 4, doubled, 4 * bond), jnp.bfloat16),
+            jax.ShapeDtypeStruct((plane // 4, doubled, 4 * bond), jnp.bfloat16),
             jax.ShapeDtypeStruct((doubled, bits), jnp.bfloat16),
-            jax.ShapeDtypeStruct((doubled, bits), jnp.float32),
+            jax.ShapeDtypeStruct((doubled, bits), jnp.bfloat16),
         ),
-        in_specs=[SMEM, SMEM] + [VMEM] * 6,
-        out_specs=(VMEM,) * 3,
+        in_specs=[SMEM] * 3 + [VMEM] * 6,
+        out_specs=(VMEM,) * 4,
         scratch_shapes=[pltpu.VMEM((depth, doubled, 2 * doubled), jnp.bfloat16)],
         compiler_params=pltpu.CompilerParams(vmem_limit_bytes=16 << 20),
         name="advance",
-    )(classes, routing, blocks, selectors, layers, left_edges, right_edges, owners)
+    )(core, classes, routing, blocks, selectors, layers, left_edges, right_edges, owners)
+    received = lax.ppermute(packed_other, "cuts_2", [(0, 1), (1, 0)])
     rows = bits * 2 // doubled
     scale = float(slots * near * plane) ** -0.5
     partial = pl.pallas_call(
         lambda *refs: amplitude_kernel(*refs, scale=scale),
         out_shape=jax.ShapeDtypeStruct((rows, doubled), jnp.float32),
-        in_specs=[VMEM] * 4,
+        in_specs=[SMEM, VMEM, VMEM, FAR, FAR, FAR],
         out_specs=VMEM,
-        scratch_shapes=[pltpu.VMEM((rows // 2, doubled), jnp.float32)] * 2,
+        scratch_shapes=[
+            pltpu.VMEM((plane, cores, bond, doubled), jnp.bfloat16),
+            pltpu.VMEM((doubled, bits), jnp.bfloat16),
+            pltpu.VMEM((doubled, bits), jnp.bfloat16),
+            pltpu.VMEM((rows // 2, doubled), jnp.float32),
+            pltpu.VMEM((rows // 2, doubled), jnp.float32),
+            pltpu.SemaphoreType.DMA((6,)),
+        ],
         compiler_params=pltpu.CompilerParams(vmem_limit_bytes=16 << 20),
         name="amplitudes",
-    )(packed, partners.reshape(slots // 4, 4 * bond, doubled), left_cols, right_cols)
+    )(
+        core,
+        packed_own,
+        received,
+        pltpu.with_memory_space_constraint(partners.reshape(plane, cores, bond, doubled), pltpu.HBM),
+        pltpu.with_memory_space_constraint(left_cols, pltpu.HBM),
+        pltpu.with_memory_space_constraint(right_cols, pltpu.HBM),
+    )
     arrived = lax.all_to_all(partial, PLANE, split_axis=0, concat_axis=0, tiled=True)
     summed = pl.pallas_call(
         fold_kernel,
@@ -180,16 +230,15 @@
         in_specs=[VMEM],
         out_specs=VMEM,
         name="fold",
-    )(arrived)
+    )(pltpu.with_memory_space_constraint(arrived, pltpu.VMEM))
     arrived = lax.all_to_all(summed, NEAR, split_axis=0, concat_axis=0, tiled=True)
-    place = lax.axis_index(NEAR).reshape(1).astype(jnp.int32)
     return pl.pallas_call(
         finish_kernel,
         out_shape=jax.ShapeDtypeStruct((2, per), jnp.float32),
         in_specs=[SMEM, VMEM],
         out_specs=VMEM,
         name="finish",
-    )(place, arrived)
+    )(place, pltpu.with_memory_space_constraint(arrived, pltpu.VMEM))
 
 
 def solution(mesh):

time: 108 us -> 106 us (0.981)
  blocking collectives: 18.5 us -> 33.8 us
  waiting for transfers between devices: 26.5 us -> 19.2 us
  local copies, waits for them, and re-layouts: 11.5 us -> 5.45 us
  starting transfers between devices: 24.9 us -> 20.4 us
    all_to_all x0 -> x1, blocking collectives: none -> 12.3 us  [on_device(): lax.all_to_all(summed, NEAR, split_axis=0, concat_axis=0, tiled=True)]
    all_to_all x2 -> x1, waiting for transfers between devices: 26.5 us -> 17 us  [on_device(): lax.all_to_all(environments.reshape(plane, cores * bond, doubled), PLANE,...]
    all_to_all x2 -> x1, starting transfers between devices: 24.9 us -> 17.5 us  [on_device(): lax.all_to_all(environments.reshape(plane, cores * bond, doubled), PLANE,...]
    unnamed x26 -> x20, local copies, waits for them, and re-layouts: 10.8 us -> 4.71 us
    all_to_all x1, blocking collectives: 18.5 us -> 21.5 us  [on_device(): lax.all_to_all(partial, PLANE, split_axis=0, concat_axis=0, tiled=True)]
    ppermute x0 -> x1, starting transfers between devices: none -> 2.85 us  [on_device(): received = lax.ppermute(packed_other, 'cuts_2', [(0, 1), (1, 0)])]
    ppermute x0 -> x1, waiting for transfers between devices: none -> 2.26 us  [on_device(): received = lax.ppermute(packed_other, 'cuts_2', [(0, 1), (1, 0)])]
    pallas_call x1, Pallas kernels: 1.62 us -> 3.28 us  [on_device(): pl.pallas_call(lambda *refs: amplitude_kernel(*refs, scale=scale), out_sh...]
where the time goes in v2:
time: 106 us; the launch traced here: 105 us
  blocking collectives  33.8 us (32%)
  Pallas kernels  26.1 us (25%)
  starting transfers between devices  20.4 us (19%)
  waiting for transfers between devices  19.2 us (18%)
  local copies, waits for them, and re-layouts  5.45 us (5%)
    pallas_call x1, Pallas kernels, on_device(): pl.pallas_call(advance_kernel, out_shape=(jax.ShapeDtypeStruct((plane //...  21.5 us
    all_to_all x1, blocking collectives, on_device(): lax.all_to_all(partial, PLANE, split_axis=0, concat_axis=0, tiled=True)  21.5 us
    all_to_all x1, starting transfers between devices, on_device(): lax.all_to_all(environments.reshape(plane, cores * bond, doubled), PLANE,...  17.5 us
    all_to_all x1, waiting for transfers between devices, on_device(): lax.all_to_all(environments.reshape(plane, cores * bond, doubled), PLANE,...  17 us
    all_to_all x1, blocking collectives, on_device(): lax.all_to_all(summed, NEAR, split_axis=0, concat_axis=0, tiled=True)  12.3 us
    unnamed x20, local copies, waits for them, and re-layouts  4.71 us
    pallas_call x1, Pallas kernels, on_device(): pl.pallas_call(lambda *refs: amplitude_kernel(*refs, scale=scale), out_sh...  3.28 us
    ppermute x1, starting transfers between devices, on_device(): received = lax.ppermute(packed_other, 'cuts_2', [(0, 1), (1, 0)])  2.85 us
  transfers between devices with their start and end apart: 2, of which 2 were waited for; matrix products, arithmetic and copies ran while one was open for 1% of the time, Pallas kernels for 20%

profile of v2, /device:TPU:1, one launch (start us, length us, event | category | flops | bytes accessed | tf_op | source)
XLA Modules:
  0.0 105.1 jit_solution(17801777951022503807)
XLA Ops:
  0.0 0.0 copy-start.9
  0.0 0.0 copy-start
  0.0 0.0 copy-start.3
  0.0 0.0 copy-start.4
  0.0 17.5 %all-to-all-start = ((bf16[64,128,128]{2,1,0:T(8,128)(2,1)}), bf16[64,128,128]{2,1,0:T(8,128)(2,1)}, u32[]{:S(2)}, u32[]{:S(2)}) async-start(bf16[64,128,128]{2,1,0:T(8,128)(2,1)} %bitcast.16), calls=%async_computation | async-start | bytes 4194304 | tf_op jit(solution)/shard_map/all_to_all | solution.py:178
  17.6 0.0 copy-done.9
  17.6 0.2 reshape.24
  17.8 0.2 copy.11
  18.0 0.4 reshape.25.owners
  18.4 0.0 copy-done
  18.4 0.0 copy-done.3
  18.4 0.0 copy-done.4
  18.4 0.0 copy-start.5
  18.4 0.7 copy-done.5
  19.1 0.0 copy-start.6
  19.1 0.7 copy-done.6
  19.8 0.0 copy-start.7
  19.8 0.7 copy-done.7
  20.5 0.0 copy-start.8
  20.5 0.7 copy-done.8
  21.1 21.5 %advance.1 = (bf16[16,128,256]{2,1,0:T(8,128)(2,1)S(1)}, bf16[16,128,256]{2,1,0:T(8,128)(2,1)S(1)}, bf16[128,4096]{1,0:T(8,128)(2,1)S(1)}, bf16[128,4096]{1,0:T(8,128)(2,1)S(1)}) custom-call(s32[1]{0:T(128)} %bitcast.core.refs_0_, s32[1,128]{1,0:T(1,128)S(1)} %copy-done.7, s32[1,128]{1,0:T(1,128)S(1)} %copy-done.8, bf16[128,64,128]{2,1,0:T(8,128)(2,1)S(1)} %copy-done, ...), custom_call_target="tpu_custom_call" | custom-call | tf_op jit(solution)/shard_map/advance/pallas_call | solution.py:186
  42.7 0.0 copy-start.1
  42.7 1.0 copy-done.1
  43.6 0.0 copy-start.2
  43.6 1.0 copy-done.2
  44.6 2.8 %collective-permute-start = (bf16[16,128,256]{2,1,0:T(8,128)(2,1)S(1)}, bf16[16,128,256]{2,1,0:T(8,128)(2,1)S(1)}, u32[]{:S(2)}, u32[]{:S(2)}) collective-permute-start(bf16[16,128,256]{2,1,0:T(8,128)(2,1)S(1)} %get-tuple-element.16), channel_id=1, source_target_pairs={{0,4},{4,0},{1,5},{5,1},{2,6},{6,2},{3,7},{7,3},{8,12},{12,8},{9,1... | collective-permute-start | bytes 3145736 | tf_op jit(solution)/shard_map/ppermute | solution.py:200
  47.5 2.3 %collective-permute-done.refs_2_ = bf16[16,128,256]{2,1,0:T(8,128)(2,1)S(1)} collective-permute-done((bf16[16,128,256]{2,1,0:T(8,128)(2,1)S(1)}, bf16[16,128,256]{2,1,0:T(8,128)(2,1)S(1)}, u32[]{:S(2)}, u32[]{:S(2)}) %collective-permute-start) | collective-permute-done | bytes 1048608 | tf_op jit(solution)/shard_map/ppermute | solution.py:200
  49.8 17.0 %all-to-all-done = bf16[64,128,128]{2,1,0:T(8,128)(2,1)} async-done(((bf16[64,128,128]{2,1,0:T(8,128)(2,1)}), bf16[64,128,128]{2,1,0:T(8,128)(2,1)}, u32[]{:S(2)}, u32[]{:S(2)}) %all-to-all-start) | async-done | bytes 2097184 | tf_op jit(solution)/shard_map/all_to_all | solution.py:178
  66.7 3.3 %amplitudes.1 = f32[64,128]{1,0:T(8,128)S(1)} custom-call(s32[1]{0:T(128)} %bitcast.core.refs_0_, bf16[16,128,256]{2,1,0:T(8,128)(2,1)S(1)} %get-tuple-element.15.refs_1_, bf16[16,128,256]{2,1,0:T(8,128)(2,1)S(1)} %collective-permute-done.refs_2_, bf16[64,2,64,128]{3,2,1,0:T(8,128)(2,1)} %bitcast.4.refs_3_, bf16[128,4096]{1,0:T(8,128)(2,1)} %copy-done.1, ...), custom_call_target="tpu_custom_call" | custom-call | tf_op jit(solution)/shard_map/amplitudes/pallas_call | solution.py:203
  70.0 21.5 %all_to_all.27 = f32[64,1,128]{2,1,0:T(1,128)S(1)} all-to-all(f32[64,1,128]{2,1,0:T(1,128)S(1)} %bitcast.13), channel_id=1, replica_groups=mesh['cuts_0'=8,'cuts_1'=8,'cuts_2'=2,'batch'=4] {'cuts_0','cuts_1'}, dimensions={0} | all-to-all | bytes 65536 | tf_op jit(solution)/shard_map/all_to_all | solution.py:226
  91.5 0.6 fold.1
  92.1 12.3 %all_to_all.28 = f32[8,1,128]{2,1,0:T(1,128)S(1)} all-to-all(f32[8,1,128]{2,1,0:T(1,128)} %bitcast.18), channel_id=1, replica_groups=mesh['cuts_0'=8,'cuts_1'=8,'cuts_2'=2,'batch'=4] {'cuts_2','batch'}, dimensions={0} | all-to-all | bytes 8192 | tf_op jit(solution)/shard_map/all_to_all | solution.py:234
  104.4 0.7 finish.1
Async XLA Ops:
  0.0 17.6 %copy-start.9 = (s32[4096]{0:T(1024)S(1)}, s32[4096]{0:T(1024)}, u32[]{:S(2)}) copy-start(s32[4096]{0:T(1024)} %param.17) | copy-start | bytes 49156
  0.0 18.4 %copy-start = (bf16[128,64,128]{2,1,0:T(8,128)(2,1)S(1)}, bf16[128,64,128]{2,1,0:T(8,128)(2,1)}, u32[]{:S(2)}) copy-start(bf16[128,64,128]{2,1,0:T(8,128)(2,1)} %blocks.1) | copy-start | bytes 6291460
  0.0 18.4 %copy-start.3 = (bf16[128,8,128]{2,1,0:T(8,128)(2,1)S(1)}, bf16[128,8,128]{2,1,0:T(8,128)(2,1)}, u32[]{:S(2)}) copy-start(bf16[128,8,128]{2,1,0:T(8,128)(2,1)} %selectors.1) | copy-start | bytes 786436
  0.0 18.4 %copy-start.4 = (bf16[8,64,128]{2,1,0:T(8,128)(2,1)S(1)}, bf16[8,64,128]{2,1,0:T(8,128)(2,1)}, u32[]{:S(2)}) copy-start(bf16[8,64,128]{2,1,0:T(8,128)(2,1)} %layers.1) | copy-start | bytes 393220
  0.0 66.7 %all-to-all-start = ((bf16[64,128,128]{2,1,0:T(8,128)(2,1)}), bf16[64,128,128]{2,1,0:T(8,128)(2,1)}, u32[]{:S(2)}, u32[]{:S(2)}) async-start(bf16[64,128,128]{2,1,0:T(8,128)(2,1)} %bitcast.16), calls=%async_computation | async-start | bytes 4194304 | tf_op jit(solution)/shard_map/all_to_all | solution.py:178
  18.4 0.7 copy-start.5
  19.1 0.7 copy-start.6
  19.8 0.7 copy-start.7
  20.5 0.7 copy-start.8
  42.7 1.0 copy-start.1
  43.6 1.0 copy-start.2
  44.6 5.1 %collective-permute-start = (bf16[16,128,256]{2,1,0:T(8,128)(2,1)S(1)}, bf16[16,128,256]{2,1,0:T(8,128)(2,1)S(1)}, u32[]{:S(2)}, u32[]{:S(2)}) collective-permute-start(bf16[16,128,256]{2,1,0:T(8,128)(2,1)S(1)} %get-tuple-element.16), channel_id=1, source_target_pairs={{0,4},{4,0},{1,5},{5,1},{2,6},{6,2},{3,7},{7,3},{8,12},{12,8},{9,1... | collective-permute-start | bytes 3145736 | tf_op jit(solution)/shard_map/ppermute | solution.py:200

commit v3 on v2

--- a/solution.py
+++ b/solution.py
@@ -23,8 +23,8 @@
 
 
 def advance_kernel(
-    core, levels, sending, blocks, selectors, layers, left, right, owners,
-    packed_other, packed_own, left_cols, right_cols, tables,
+    core, levels, sending, blocks, selectors, layers, left, owners,
+    packed_other, packed_own, left_cols, tables,
 ):
     depth, bond, doubled = layers.shape
     pairs = blocks.shape[0] // 2
@@ -36,11 +36,7 @@
         tables[layer, bond:, :doubled] = turned.astype(jnp.bfloat16)
         tables[layer, bond:, doubled:] = (-plain).astype(jnp.bfloat16)
 
-    def stacked(edges):
-        return jnp.concatenate([edges[:, :bond], edges[:, bond:]], axis=0)
-
-    left_rows = stacked(left[...])
-    right_rows = stacked(right[...])
+    left_rows = jnp.concatenate([left[:, :bond], left[:, bond:]], axis=0)
     width = 512
 
     def columns(step, carry):
@@ -48,9 +44,7 @@
         owner = owners[:, at]
         codes = lax.broadcasted_iota(jnp.int32, (bond, width), 0)
         by_left = jnp.where(codes == owner // bond, 1.0, 0.0).astype(jnp.bfloat16)
-        by_right = jnp.where(codes == owner % bond, 1.0, 0.0).astype(jnp.bfloat16)
         left_cols[:, at] = jnp.dot(left_rows, by_left, preferred_element_type=jnp.float32).astype(jnp.bfloat16)
-        right_cols[:, at] = jnp.dot(right_rows, by_right, preferred_element_type=jnp.float32).astype(jnp.bfloat16)
         return carry
 
     lax.fori_loop(0, owners.shape[1] // width, columns, 0)
@@ -95,50 +89,47 @@
     lax.fori_loop(0, steps, lambda i, c: group(i, c, core[0], packed_own), 0)
 
 
+def split(matrix):
+    high = matrix.astype(jnp.bfloat16)
+    return high, (matrix - high.astype(jnp.float32)).astype(jnp.bfloat16)
+
+
 def amplitude_kernel(
-    core, own, other, partners_far, left_far, right_far, partial,
-    partners, left_cols, right_cols, real_rows, imag_rows, arrivals, *, scale,
+    core, own, partners, owners, other_far, left_far, right_far, partial,
+    other, left_cols, right, real_rows, imag_rows, arrivals, *, scale,
 ):
     quads, doubled, depth = own.shape
     bond = doubled // 2
-    parts = 4
-    each = quads // parts
-
-    def load(part):
-        at = pl.ds(part * each * 4, each * 4)
-        return pltpu.make_async_copy(partners_far.at[at], partners.at[at], arrivals.at[part])
-
-    for part in range(parts):
-        load(part).start()
-    edges = (
-        pltpu.make_async_copy(left_far, left_cols, arrivals.at[parts]),
-        pltpu.make_async_copy(right_far, right_cols, arrivals.at[parts + 1]),
-    )
-    for edge in edges:
-        edge.start()
+    fetch_other = pltpu.make_async_copy(other_far, other, arrivals.at[0])
+    fetch_left = pltpu.make_async_copy(left_far, left_cols, arrivals.at[1])
+    fetch_right = pltpu.make_async_copy(right_far, right, arrivals.at[2])
+    fetch_other.start()
+    fetch_right.start()
+    fetch_left.start()
     total = jnp.zeros((doubled, doubled), jnp.float32)
-    for part in range(parts):
-        load(part).wait()
-        for quad in range(part * each, (part + 1) * each):
-            for worked, side in ((own, core[0]), (other, 1 - core[0])):
-                rows = jnp.concatenate([partners[quad * 4 + k, side] for k in range(4)], axis=0)
-                total = total + jnp.dot(worked[quad], rows, preferred_element_type=jnp.float32)
-    core_matrix = (total[:bond] + times_i(total[bond:])) * scale
-    whole = jnp.concatenate([core_matrix, times_i(core_matrix)], axis=0)
-    high = whole.astype(jnp.bfloat16)
-    low = (whole - high.astype(jnp.float32)).astype(jnp.bfloat16)
+    for worked, side in ((own, core[0]), (other, 1 - core[0])):
+        if worked is other:
+            fetch_other.wait()
+        for quad in range(quads):
+            rows = jnp.concatenate([partners[quad * 4 + k, side] for k in range(4)], axis=0)
+            total = total + jnp.dot(worked[quad], rows, preferred_element_type=jnp.float32)
+    whole = (total[:bond] + times_i(total[bond:])) * scale
+    fetch_right.wait()
+    plain = right[...].astype(jnp.float32)
+    factors = jnp.concatenate([plain, times_i(plain)], axis=0).astype(jnp.bfloat16)
+    waves = jnp.dot(jnp.concatenate(split(whole), axis=0), factors, preferred_element_type=jnp.float32)
+    wave = waves[:bond] + waves[bond:]
+    high, low = split(jnp.concatenate([wave, times_i(wave)], axis=0))
     pieces = jnp.concatenate([high.astype(jnp.float32), low.astype(jnp.float32)], axis=0).T.astype(jnp.bfloat16)
     width = 512
-    for edge in edges:
-        edge.wait()
+    fetch_left.wait()
     for start in range(0, left_cols.shape[1], width):
         cols = left_cols[:, start : start + width]
         half = jnp.dot(pieces, jnp.concatenate([cols, cols], axis=0), preferred_element_type=jnp.float32)
-        half_real, half_imag = half[:bond], half[bond:]
-        right_real = right_cols[:bond, start : start + width].astype(jnp.float32)
-        right_imag = right_cols[bond:, start : start + width].astype(jnp.float32)
-        real = jnp.sum(half_real * right_real - half_imag * right_imag, axis=0, keepdims=True)
-        imag = jnp.sum(half_real * right_imag + half_imag * right_real, axis=0, keepdims=True)
+        codes = lax.broadcasted_iota(jnp.int32, (bond, width), 0)
+        chosen = codes == owners[:, start : start + width] % bond
+        real = jnp.sum(jnp.where(chosen, half[:bond], 0.0), axis=0, keepdims=True)
+        imag = jnp.sum(jnp.where(chosen, half[bond:], 0.0), axis=0, keepdims=True)
         for tile in range(width // 128):
             row = start // 128 + tile
             real_rows[row : row + 1, :] = real[:, tile * 128 : (tile + 1) * 128]
@@ -183,45 +174,45 @@
     per = bits // (near * plane)
     owners = owner_map.reshape(2, plane // 2, near, per).transpose(1, 2, 0, 3).reshape(1, bits)
     core, place, owners = lax.optimization_barrier((core, place, owners))
-    packed_other, packed_own, left_cols, right_cols = pl.pallas_call(
+    packed_other, packed_own, left_cols = pl.pallas_call(
         advance_kernel,
         out_shape=(
             jax.ShapeDtypeStruct((plane // 4, doubled, 4 * bond), jnp.bfloat16),
             jax.ShapeDtypeStruct((plane // 4, doubled, 4 * bond), jnp.bfloat16),
             jax.ShapeDtypeStruct((doubled, bits), jnp.bfloat16),
-            jax.ShapeDtypeStruct((doubled, bits), jnp.bfloat16),
         ),
-        in_specs=[SMEM] * 3 + [VMEM] * 6,
-        out_specs=(VMEM,) * 4,
+        in_specs=[SMEM] * 3 + [VMEM] * 5,
+        out_specs=(VMEM,) * 3,
         scratch_shapes=[pltpu.VMEM((depth, doubled, 2 * doubled), jnp.bfloat16)],
         compiler_params=pltpu.CompilerParams(vmem_limit_bytes=16 << 20),
         name="advance",
-    )(core, classes, routing, blocks, selectors, layers, left_edges, right_edges, owners)
+    )(core, classes, routing, blocks, selectors, layers, left_edges, owners)
     received = lax.ppermute(packed_other, "cuts_2", [(0, 1), (1, 0)])
     rows = bits * 2 // doubled
     scale = float(slots * near * plane) ** -0.5
     partial = pl.pallas_call(
         lambda *refs: amplitude_kernel(*refs, scale=scale),
         out_shape=jax.ShapeDtypeStruct((rows, doubled), jnp.float32),
-        in_specs=[SMEM, VMEM, VMEM, FAR, FAR, FAR],
+        in_specs=[SMEM, VMEM, VMEM, VMEM, FAR, FAR, FAR],
         out_specs=VMEM,
         scratch_shapes=[
-            pltpu.VMEM((plane, cores, bond, doubled), jnp.bfloat16),
+            pltpu.VMEM((plane // 4, doubled, 4 * bond), jnp.bfloat16),
             pltpu.VMEM((doubled, bits), jnp.bfloat16),
-            pltpu.VMEM((doubled, bits), jnp.bfloat16),
+            pltpu.VMEM(right_edges.shape, jnp.bfloat16),
             pltpu.VMEM((rows // 2, doubled), jnp.float32),
             pltpu.VMEM((rows // 2, doubled), jnp.float32),
-            pltpu.SemaphoreType.DMA((6,)),
+            pltpu.SemaphoreType.DMA((3,)),
         ],
         compiler_params=pltpu.CompilerParams(vmem_limit_bytes=16 << 20),
         name="amplitudes",
     )(
         core,
         packed_own,
-        received,
-        pltpu.with_memory_space_constraint(partners.reshape(plane, cores, bond, doubled), pltpu.HBM),
+        partners.reshape(plane, cores, bond, doubled),
+        owners,
+        pltpu.with_memory_space_constraint(received, pltpu.HBM),
         pltpu.with_memory_space_constraint(left_cols, pltpu.HBM),
-        pltpu.with_memory_space_constraint(right_cols, pltpu.HBM),
+        pltpu.with_memory_space_constraint(right_edges, pltpu.HBM),
     )
     arrived = lax.all_to_all(partial, PLANE, split_axis=0, concat_axis=0, tiled=True)
     summed = pl.pallas_call(

time: 106 us -> 105 us (level)
    unnamed x20 -> x16, local copies, waits for them, and re-layouts: 4.71 us -> 4.62 us
where the time goes in v3:
time: 105 us
  blocking collectives  33.8 us (32%)
  Pallas kernels  25.6 us (24%)
  starting transfers between devices  20.1 us (19%)
  waiting for transfers between devices  19.8 us (19%)
  local copies, waits for them, and re-layouts  5.35 us (5%)
    all_to_all x1, blocking collectives, on_device(): lax.all_to_all(partial, PLANE, split_axis=0, concat_axis=0, tiled=True)  21.4 us
    pallas_call x1, Pallas kernels, on_device(): pl.pallas_call(advance_kernel, out_shape=(jax.ShapeDtypeStruct((plane //...  21.2 us
    all_to_all x1, waiting for transfers between devices, on_device(): lax.all_to_all(environments.reshape(plane, cores * bond, doubled), PLANE,...  17.4 us
    all_to_all x1, starting transfers between devices, on_device(): lax.all_to_all(environments.reshape(plane, cores * bond, doubled), PLANE,...  17.3 us
    all_to_all x1, blocking collectives, on_device(): lax.all_to_all(summed, NEAR, split_axis=0, concat_axis=0, tiled=True)  12.3 us
    unnamed x16, local copies, waits for them, and re-layouts  4.62 us
    pallas_call x1, Pallas kernels, on_device(): pl.pallas_call(lambda *refs: amplitude_kernel(*refs, scale=scale), out_sh...  3.05 us
    ppermute x1, starting transfers between devices, on_device(): received = lax.ppermute(packed_other, 'cuts_2', [(0, 1), (1, 0)])  2.84 us
  transfers between devices with their start and end apart: 2, of which 2 were waited for; matrix products, arithmetic and copies ran while one was open for 1% of the time, Pallas kernels for 20%

profile of v3, /device:TPU:1, one launch (start us, length us, event | category | flops | bytes accessed | tf_op | source)
XLA Modules:
  0.0 104.7 jit_solution(15726599536314786463)
XLA Ops:
  0.0 0.0 copy-start.7
  0.0 0.0 copy-start.2
  0.0 0.0 copy-start.3
  0.0 17.3 %all-to-all-start = ((bf16[64,128,128]{2,1,0:T(8,128)(2,1)}), bf16[64,128,128]{2,1,0:T(8,128)(2,1)S(1)}, u32[]{:S(2)}, u32[]{:S(2)}) async-start(bf16[64,128,128]{2,1,0:T(8,128)(2,1)} %bitcast.17), calls=%async_computation | async-start | bytes 4194304 | tf_op jit(solution)/shard_map/all_to_all | solution.py:169
  17.3 0.0 copy-done.7
  17.3 0.2 reshape.24
  17.5 0.2 copy.11
  17.7 0.4 reshape.25.owners.refs_3_
  18.1 0.0 copy-done.2
  18.1 0.0 copy-done.3
  18.1 0.0 copy-start
  18.1 1.6 %copy-done = bf16[128,64,128]{2,1,0:T(8,128)(2,1)S(1)} copy-done((bf16[128,64,128]{2,1,0:T(8,128)(2,1)S(1)}, bf16[128,64,128]{2,1,0:T(8,128)(2,1)}, u32[]{:S(2)}) %copy-start) | copy-done | bytes 2097176
  19.7 0.0 copy-start.4
  19.7 0.7 copy-done.4
  20.4 0.0 copy-start.5
  20.4 0.7 copy-done.5
  21.1 0.0 copy-start.6
  21.1 0.7 copy-done.6
  21.7 21.2 %advance.1 = (bf16[16,128,256]{2,1,0:T(8,128)(2,1)S(1)}, bf16[16,128,256]{2,1,0:T(8,128)(2,1)S(1)}, bf16[128,4096]{1,0:T(8,128)(2,1)S(1)}) custom-call(s32[1]{0:T(128)} %bitcast.core.refs_0_, s32[1,128]{1,0:T(1,128)S(1)} %copy-done.5, s32[1,128]{1,0:T(1,128)S(1)} %copy-done.6, bf16[128,64,128]{2,1,0:T(8,128)(2,1)S(1)} %copy-done, ...), custom_call_target="tpu_custom_call" | custom-call | tf_op jit(solution)/shard_map/advance/pallas_call | solution.py:177
  43.0 0.0 copy-start.1
  43.0 1.0 copy-done.1
  44.0 2.8 %collective-permute-start = (bf16[16,128,256]{2,1,0:T(8,128)(2,1)S(1)}, bf16[16,128,256]{2,1,0:T(8,128)(2,1)}, u32[]{:S(2)}, u32[]{:S(2)}) collective-permute-start(bf16[16,128,256]{2,1,0:T(8,128)(2,1)S(1)} %get-tuple-element.15), channel_id=1, source_target_pairs={{0,4},{4,0},{1,5},{5,1},{2,6},{6,2},{3,7},{7,3},{8,12},{12,8},{9,1... | collective-permute-start | bytes 3145736 | tf_op jit(solution)/shard_map/ppermute | solution.py:190
  46.8 2.4 %collective-permute-done.refs_4_ = bf16[16,128,256]{2,1,0:T(8,128)(2,1)} collective-permute-done((bf16[16,128,256]{2,1,0:T(8,128)(2,1)S(1)}, bf16[16,128,256]{2,1,0:T(8,128)(2,1)}, u32[]{:S(2)}, u32[]{:S(2)}) %collective-permute-start) | collective-permute-done | bytes 1048608 | tf_op jit(solution)/shard_map/ppermute | solution.py:190
  49.2 17.4 %all-to-all-done = bf16[64,128,128]{2,1,0:T(8,128)(2,1)S(1)} async-done(((bf16[64,128,128]{2,1,0:T(8,128)(2,1)}), bf16[64,128,128]{2,1,0:T(8,128)(2,1)S(1)}, u32[]{:S(2)}, u32[]{:S(2)}) %all-to-all-start) | async-done | bytes 2097184 | tf_op jit(solution)/shard_map/all_to_all | solution.py:169
  66.6 3.0 %amplitudes.1 = f32[64,128]{1,0:T(8,128)S(1)} custom-call(s32[1]{0:T(128)} %bitcast.core.refs_0_, bf16[16,128,256]{2,1,0:T(8,128)(2,1)S(1)} %get-tuple-element.14.refs_1_, bf16[64,2,64,128]{3,2,1,0:T(8,128)(2,1)S(1)} %bitcast.13, s32[1,4096]{1,0:T(1,128)S(1)} %reshape.25.owners.refs_3_, bf16[16,128,256]{2,1,0:T(8,128)(2,1)} %collective-permute-done.refs_4_, ...), custom_call_target="tpu_custom_call" | custom-call | tf_op jit(solution)/shard_map/amplitudes/pallas_call | solution.py:193
  69.7 21.4 %all_to_all.27 = f32[64,1,128]{2,1,0:T(1,128)S(1)} all-to-all(f32[64,1,128]{2,1,0:T(1,128)S(1)} %bitcast.14), channel_id=1, replica_groups=mesh['cuts_0'=8,'cuts_1'=8,'cuts_2'=2,'batch'=4] {'cuts_0','cuts_1'}, dimensions={0} | all-to-all | bytes 65536 | tf_op jit(solution)/shard_map/all_to_all | solution.py:217
  91.1 0.6 fold.1
  91.7 12.3 %all_to_all.28 = f32[8,1,128]{2,1,0:T(1,128)S(1)} all-to-all(f32[8,1,128]{2,1,0:T(1,128)} %bitcast.19), channel_id=1, replica_groups=mesh['cuts_0'=8,'cuts_1'=8,'cuts_2'=2,'batch'=4] {'cuts_2','batch'}, dimensions={0} | all-to-all | bytes 8192 | tf_op jit(solution)/shard_map/all_to_all | solution.py:225
  104.0 0.7 finish.1
Async XLA Ops:
  0.0 17.3 %copy-start.7 = (s32[4096]{0:T(1024)S(1)}, s32[4096]{0:T(1024)}, u32[]{:S(2)}) copy-start(s32[4096]{0:T(1024)} %param.17) | copy-start | bytes 49156
  0.0 18.1 %copy-start.2 = (bf16[128,8,128]{2,1,0:T(8,128)(2,1)S(1)}, bf16[128,8,128]{2,1,0:T(8,128)(2,1)}, u32[]{:S(2)}) copy-start(bf16[128,8,128]{2,1,0:T(8,128)(2,1)} %selectors.1) | copy-start | bytes 786436
  0.0 18.1 %copy-start.3 = (bf16[8,64,128]{2,1,0:T(8,128)(2,1)S(1)}, bf16[8,64,128]{2,1,0:T(8,128)(2,1)}, u32[]{:S(2)}) copy-start(bf16[8,64,128]{2,1,0:T(8,128)(2,1)} %layers.1) | copy-start | bytes 393220
  0.0 66.6 %all-to-all-start = ((bf16[64,128,128]{2,1,0:T(8,128)(2,1)}), bf16[64,128,128]{2,1,0:T(8,128)(2,1)S(1)}, u32[]{:S(2)}, u32[]{:S(2)}) async-start(bf16[64,128,128]{2,1,0:T(8,128)(2,1)} %bitcast.17), calls=%async_computation | async-start | bytes 4194304 | tf_op jit(solution)/shard_map/all_to_all | solution.py:169
  18.1 1.6 %copy-start = (bf16[128,64,128]{2,1,0:T(8,128)(2,1)S(1)}, bf16[128,64,128]{2,1,0:T(8,128)(2,1)}, u32[]{:S(2)}) copy-start(bf16[128,64,128]{2,1,0:T(8,128)(2,1)} %blocks.1) | copy-start | bytes 6291460
  19.7 0.7 copy-start.4
  20.4 0.7 copy-start.5
  21.1 0.7 copy-start.6
  43.0 1.0 copy-start.1
  44.0 5.2 %collective-permute-start = (bf16[16,128,256]{2,1,0:T(8,128)(2,1)S(1)}, bf16[16,128,256]{2,1,0:T(8,128)(2,1)}, u32[]{:S(2)}, u32[]{:S(2)}) collective-permute-start(bf16[16,128,256]{2,1,0:T(8,128)(2,1)S(1)} %get-tuple-element.15), channel_id=1, source_target_pairs={{0,4},{4,0},{1,5},{5,1},{2,6},{6,2},{3,7},{7,3},{8,12},{12,8},{9,1... | collective-permute-start | bytes 3145736 | tf_op jit(solution)/shard_map/ppermute | solution.py:190

commit v4 on v3

--- a/solution.py
+++ b/solution.py
@@ -11,6 +11,7 @@
 PLANE = ("cuts_0", "cuts_1")
 NEAR = ("cuts_2", "batch")
 TOGETHER = 8
+PARTS = 4
 
 
 def lower_half(shape):
@@ -23,7 +24,7 @@
 
 
 def advance_kernel(
-    core, levels, sending, blocks, selectors, layers, left, owners,
+    core, levels, sending, blocks, selectors, layers, left, right, owners,
     packed_other, packed_own, left_cols, tables,
 ):
     depth, bond, doubled = layers.shape
@@ -36,6 +37,8 @@
         tables[layer, bond:, :doubled] = turned.astype(jnp.bfloat16)
         tables[layer, bond:, doubled:] = (-plain).astype(jnp.bfloat16)
 
+    plain = right[...].astype(jnp.float32)
+    packed_own[pairs // 4, :, :doubled] = jnp.concatenate([plain, times_i(plain)], axis=0).astype(jnp.bfloat16)
     left_rows = jnp.concatenate([left[:, :bond], left[:, bond:]], axis=0)
     width = 512
 
@@ -95,34 +98,31 @@
 
 
 def amplitude_kernel(
-    core, own, partners, owners, other_far, left_far, right_far, partial,
-    other, left_cols, right, real_rows, imag_rows, arrivals, *, scale,
+    core, own, partners, owners, other_far, left_far, partial,
+    other, left_cols, real_rows, imag_rows, arrivals, *, scale,
 ):
-    quads, doubled, depth = own.shape
+    quads, doubled, depth = other.shape
     bond = doubled // 2
-    fetch_other = pltpu.make_async_copy(other_far, other, arrivals.at[0])
-    fetch_left = pltpu.make_async_copy(left_far, left_cols, arrivals.at[1])
-    fetch_right = pltpu.make_async_copy(right_far, right, arrivals.at[2])
-    fetch_other.start()
-    fetch_right.start()
-    fetch_left.start()
+    for far, near, arrival in ((other_far, other, 0), (left_far, left_cols, 1)):
+        each = near.shape[0] // PARTS
+        for part in range(PARTS):
+            at = pl.ds(part * each, each)
+            pltpu.make_async_copy(far.at[at], near.at[at], arrivals.at[arrival]).start()
     total = jnp.zeros((doubled, doubled), jnp.float32)
     for worked, side in ((own, core[0]), (other, 1 - core[0])):
         if worked is other:
-            fetch_other.wait()
+            pltpu.make_async_copy(other_far, other, arrivals.at[0]).wait()
         for quad in range(quads):
             rows = jnp.concatenate([partners[quad * 4 + k, side] for k in range(4)], axis=0)
             total = total + jnp.dot(worked[quad], rows, preferred_element_type=jnp.float32)
     whole = (total[:bond] + times_i(total[bond:])) * scale
-    fetch_right.wait()
-    plain = right[...].astype(jnp.float32)
-    factors = jnp.concatenate([plain, times_i(plain)], axis=0).astype(jnp.bfloat16)
+    factors = own[quads, :, :doubled]
     waves = jnp.dot(jnp.concatenate(split(whole), axis=0), factors, preferred_element_type=jnp.float32)
     wave = waves[:bond] + waves[bond:]
     high, low = split(jnp.concatenate([wave, times_i(wave)], axis=0))
     pieces = jnp.concatenate([high.astype(jnp.float32), low.astype(jnp.float32)], axis=0).T.astype(jnp.bfloat16)
     width = 512
-    fetch_left.wait()
+    pltpu.make_async_copy(left_far, left_cols, arrivals.at[1]).wait()
     for start in range(0, left_cols.shape[1], width):
         cols = left_cols[:, start : start + width]
         half = jnp.dot(pieces, jnp.concatenate([cols, cols], axis=0), preferred_element_type=jnp.float32)
@@ -141,10 +141,6 @@
     partial[half_rows:] = jnp.where(first, pltpu.roll(real, 120, axis=1), imag)
 
 
-def fold_kernel(arrived, summed):
-    summed[...] = jnp.broadcast_to(jnp.sum(arrived[...], axis=0, keepdims=True), summed.shape)
-
-
 def finish_kernel(place, arrived, out):
     total = jnp.broadcast_to(jnp.sum(arrived[...], axis=0, keepdims=True), (8, 128))
     total = pltpu.roll(total, (128 - 16 * place[0]) % 128, axis=1)
@@ -178,30 +174,29 @@
         advance_kernel,
         out_shape=(
             jax.ShapeDtypeStruct((plane // 4, doubled, 4 * bond), jnp.bfloat16),
-            jax.ShapeDtypeStruct((plane // 4, doubled, 4 * bond), jnp.bfloat16),
+            jax.ShapeDtypeStruct((plane // 4 + 1, doubled, 4 * bond), jnp.bfloat16),
             jax.ShapeDtypeStruct((doubled, bits), jnp.bfloat16),
         ),
-        in_specs=[SMEM] * 3 + [VMEM] * 5,
+        in_specs=[SMEM] * 3 + [VMEM] * 6,
         out_specs=(VMEM,) * 3,
         scratch_shapes=[pltpu.VMEM((depth, doubled, 2 * doubled), jnp.bfloat16)],
         compiler_params=pltpu.CompilerParams(vmem_limit_bytes=16 << 20),
         name="advance",
-    )(core, classes, routing, blocks, selectors, layers, left_edges, owners)
+    )(core, classes, routing, blocks, selectors, layers, left_edges, right_edges, owners)
     received = lax.ppermute(packed_other, "cuts_2", [(0, 1), (1, 0)])
     rows = bits * 2 // doubled
     scale = float(slots * near * plane) ** -0.5
     partial = pl.pallas_call(
         lambda *refs: amplitude_kernel(*refs, scale=scale),
         out_shape=jax.ShapeDtypeStruct((rows, doubled), jnp.float32),
-        in_specs=[SMEM, VMEM, VMEM, VMEM, FAR, FAR, FAR],
+        in_specs=[SMEM, VMEM, VMEM, VMEM, FAR, FAR],
         out_specs=VMEM,
         scratch_shapes=[
             pltpu.VMEM((plane // 4, doubled, 4 * bond), jnp.bfloat16),
             pltpu.VMEM((doubled, bits), jnp.bfloat16),
-            pltpu.VMEM(right_edges.shape, jnp.bfloat16),
             pltpu.VMEM((rows // 2, doubled), jnp.float32),
             pltpu.VMEM((rows // 2, doubled), jnp.float32),
-            pltpu.SemaphoreType.DMA((3,)),
+            pltpu.SemaphoreType.DMA((2,)),
         ],
         compiler_params=pltpu.CompilerParams(vmem_limit_bytes=16 << 20),
         name="amplitudes",
@@ -212,17 +207,9 @@
         owners,
         pltpu.with_memory_space_constraint(received, pltpu.HBM),
         pltpu.with_memory_space_constraint(left_cols, pltpu.HBM),
-        pltpu.with_memory_space_constraint(right_edges, pltpu.HBM),
-    )
-    arrived = lax.all_to_all(partial, PLANE, split_axis=0, concat_axis=0, tiled=True)
-    summed = pl.pallas_call(
-        fold_kernel,
-        out_shape=jax.ShapeDtypeStruct((near, doubled), jnp.float32),
-        in_specs=[VMEM],
-        out_specs=VMEM,
-        name="fold",
-    )(pltpu.with_memory_space_constraint(arrived, pltpu.VMEM))
-    arrived = lax.all_to_all(summed, NEAR, split_axis=0, concat_axis=0, tiled=True)
+    )
+    sent = jnp.broadcast_to(partial[:, None, :], (plane, near, doubled)).reshape(plane * near, doubled)
+    arrived = lax.all_to_all(sent, CUTS_BATCH, split_axis=0, concat_axis=0, tiled=True)
     return pl.pallas_call(
         finish_kernel,
         out_shape=jax.ShapeDtypeStruct((2, per), jnp.float32),

time: 105 us -> 104 us (level)
  waiting for transfers between devices: 19.8 us -> 20.9 us
  local copies, waits for them, and re-layouts: 5.35 us -> 4.27 us
    unnamed x16 -> x18, local copies, waits for them, and re-layouts: 4.62 us -> 3.51 us
    all_to_all x1, waiting for transfers between devices: 17.4 us -> 18.5 us  [on_device(): lax.all_to_all(environments.reshape(plane, cores * bond, doubled), PLANE,...]
    all_to_all x2 -> x1, blocking collectives: 33.8 us -> 33.5 us  [on_device(): lax.all_to_all(sent, CUTS_BATCH, split_axis=0, concat_axis=0, tiled=True)]
  transfers between devices with their start and end apart: 2 -> 2, of which waited for: 2 -> 2; matrix products, arithmetic and copies ran while one was open for 1% -> 1% of each run, Pallas kernels for 20% -> 21%
where the time goes in v4:
time: 104 us
  blocking collectives  33.5 us (32%)
  Pallas kernels  24.6 us (24%)
  waiting for transfers between devices  20.9 us (20%)
  starting transfers between devices  20.1 us (19%)
  local copies, waits for them, and re-layouts  4.27 us (4%)
    all_to_all x1, blocking collectives, on_device(): lax.all_to_all(sent, CUTS_BATCH, split_axis=0, concat_axis=0, tiled=True)  33.5 us
    pallas_call x1, Pallas kernels, on_device(): pl.pallas_call(advance_kernel, out_shape=(jax.ShapeDtypeStruct((plane //...  21.2 us
    all_to_all x1, waiting for transfers between devices, on_device(): lax.all_to_all(environments.reshape(plane, cores * bond, doubled), PLANE,...  18.5 us
    all_to_all x1, starting transfers between devices, on_device(): lax.all_to_all(environments.reshape(plane, cores * bond, doubled), PLANE,...  17.3 us
    unnamed x18, local copies, waits for them, and re-layouts  3.51 us
    ppermute x1, starting transfers between devices, on_device(): received = lax.ppermute(packed_other, 'cuts_2', [(0, 1), (1, 0)])  2.86 us
    pallas_call x1, Pallas kernels, on_device(): pl.pallas_call(lambda *refs: amplitude_kernel(*refs, scale=scale), out_sh...  2.59 us
    ppermute x1, waiting for transfers between devices, on_device(): received = lax.ppermute(packed_other, 'cuts_2', [(0, 1), (1, 0)])  2.4 us
  transfers between devices with their start and end apart: 2, of which 2 were waited for; matrix products, arithmetic and copies ran while one was open for 1% of the time, Pallas kernels for 21%

profile of v4, /device:TPU:1, one launch (start us, length us, event | category | flops | bytes accessed | tf_op | source)
XLA Modules:
  0.0 103.5 jit_solution(12178553004641486974)
XLA Ops:
  0.0 0.0 copy-start.8
  0.0 0.0 copy-start.2
  0.0 0.0 copy-start.4
  0.0 0.0 copy-start.5
  0.0 0.0 copy-start.6
  0.0 0.0 copy-start.7
  0.0 17.3 %all-to-all-start = ((bf16[64,128,128]{2,1,0:T(8,128)(2,1)}), bf16[64,128,128]{2,1,0:T(8,128)(2,1)S(1)}, u32[]{:S(2)}, u32[]{:S(2)}) async-start(bf16[64,128,128]{2,1,0:T(8,128)(2,1)} %bitcast.9), calls=%async_computation | async-start | bytes 4194304 | tf_op jit(solution)/shard_map/all_to_all | solution.py:165
  17.3 0.0 copy-done.8
  17.3 0.2 reshape.25
  17.5 0.2 copy.11
  17.7 0.4 reshape.26.owners.refs_3_
  18.1 0.0 copy-done.2
  18.1 0.0 copy-done.4
  18.1 0.0 copy-done.5
  18.1 0.0 copy-done.6
  18.2 0.0 copy-done.7
  18.2 0.0 copy-start
  18.2 1.6 %copy-done = bf16[128,64,128]{2,1,0:T(8,128)(2,1)S(1)} copy-done((bf16[128,64,128]{2,1,0:T(8,128)(2,1)S(1)}, bf16[128,64,128]{2,1,0:T(8,128)(2,1)}, u32[]{:S(2)}) %copy-start) | copy-done | bytes 2097176
  19.8 0.0 copy-start.3
  19.8 0.9 copy-done.3
  20.7 21.2 %advance.1 = (bf16[16,128,256]{2,1,0:T(8,128)(2,1)S(1)}, bf16[17,128,256]{2,1,0:T(8,128)(2,1)S(1)}, bf16[128,4096]{1,0:T(8,128)(2,1)S(1)}) custom-call(s32[1]{0:T(128)} %bitcast.core.refs_0_, s32[1,128]{1,0:T(1,128)S(1)} %copy-done.6, s32[1,128]{1,0:T(1,128)S(1)} %copy-done.7, bf16[128,64,128]{2,1,0:T(8,128)(2,1)S(1)} %copy-done, ...), custom_call_target="tpu_custom_call" | custom-call | tf_op jit(solution)/shard_map/advance/pallas_call | solution.py:173
  41.9 0.0 copy-start.1
  41.9 1.0 copy-done.1
  42.9 2.9 %collective-permute-start = (bf16[16,128,256]{2,1,0:T(8,128)(2,1)S(1)}, bf16[16,128,256]{2,1,0:T(8,128)(2,1)}, u32[]{:S(2)}, u32[]{:S(2)}) collective-permute-start(bf16[16,128,256]{2,1,0:T(8,128)(2,1)S(1)} %get-tuple-element.15), channel_id=1, source_target_pairs={{0,4},{4,0},{1,5},{5,1},{2,6},{6,2},{3,7},{7,3},{8,12},{12,8},{9,1... | collective-permute-start | bytes 3145736 | tf_op jit(solution)/shard_map/ppermute | solution.py:186
  45.8 2.4 %collective-permute-done.refs_4_ = bf16[16,128,256]{2,1,0:T(8,128)(2,1)} collective-permute-done((bf16[16,128,256]{2,1,0:T(8,128)(2,1)S(1)}, bf16[16,128,256]{2,1,0:T(8,128)(2,1)}, u32[]{:S(2)}, u32[]{:S(2)}) %collective-permute-start) | collective-permute-done | bytes 1048608 | tf_op jit(solution)/shard_map/ppermute | solution.py:186
  48.2 18.5 %all-to-all-done = bf16[64,128,128]{2,1,0:T(8,128)(2,1)S(1)} async-done(((bf16[64,128,128]{2,1,0:T(8,128)(2,1)}), bf16[64,128,128]{2,1,0:T(8,128)(2,1)S(1)}, u32[]{:S(2)}, u32[]{:S(2)}) %all-to-all-start) | async-done | bytes 2097184 | tf_op jit(solution)/shard_map/all_to_all | solution.py:165
  66.6 2.6 %amplitudes.1 = f32[64,128]{1,0:T(8,128)S(1)} custom-call(s32[1]{0:T(128)} %bitcast.core.refs_0_, bf16[17,128,256]{2,1,0:T(8,128)(2,1)S(1)} %get-tuple-element.14.refs_1_, bf16[64,2,64,128]{3,2,1,0:T(8,128)(2,1)S(1)} %bitcast.7, s32[1,4096]{1,0:T(1,128)S(1)} %reshape.26.owners.refs_3_, bf16[16,128,256]{2,1,0:T(8,128)(2,1)} %collective-permute-done.refs_4_, ...), custom_call_target="tpu_custom_call" | custom-call | tf_op jit(solution)/shard_map/amplitudes/pallas_call | solution.py:189
  69.3 33.5 %all_to_all.16 = f32[512,1,128]{2,1,0:T(1,128)S(1)} all-to-all(f32[512,1,128]{2,1,0:T(1,128)S(1)} %bitcast.10), channel_id=1, replica_groups=mesh['cuts_0'=8,'cuts_1'=8,'cuts_2'=2,'batch'=4] {'cuts_0','cuts_1','cut..., dimensions={0} | all-to-all | bytes 524288 | tf_op jit(solution)/shard_map/all_to_all | solution.py:212
  102.7 0.8 finish.1
  (1 shorter events, 0.0 us)
Async XLA Ops:
  0.0 17.3 %copy-start.8 = (s32[4096]{0:T(1024)S(1)}, s32[4096]{0:T(1024)}, u32[]{:S(2)}) copy-start(s32[4096]{0:T(1024)} %param.17) | copy-start | bytes 49156
  0.0 18.1 %copy-start.2 = (bf16[128,8,128]{2,1,0:T(8,128)(2,1)S(1)}, bf16[128,8,128]{2,1,0:T(8,128)(2,1)}, u32[]{:S(2)}) copy-start(bf16[128,8,128]{2,1,0:T(8,128)(2,1)} %selectors.1) | copy-start | bytes 786436
  0.0 18.1 %copy-start.4 = (bf16[64,128]{1,0:T(8,128)(2,1)S(1)}, bf16[64,128]{1,0:T(8,128)(2,1)}, u32[]{:S(2)}) copy-start(bf16[64,128]{1,0:T(8,128)(2,1)} %left.1) | copy-start | bytes 49156
  0.0 18.1 %copy-start.5 = (bf16[64,128]{1,0:T(8,128)(2,1)S(1)}, bf16[64,128]{1,0:T(8,128)(2,1)}, u32[]{:S(2)}) copy-start(bf16[64,128]{1,0:T(8,128)(2,1)} %right.1) | copy-start | bytes 49156
  0.0 18.1 %copy-start.6 = (s32[1,128]{1,0:T(1,128)S(1)}, s32[1,128]{1,0:T(1,128)}, u32[]{:S(2)}) copy-start(s32[1,128]{1,0:T(1,128)} %levels.1) | copy-start | bytes 1540
  0.0 18.1 %copy-start.7 = (s32[1,128]{1,0:T(1,128)S(1)}, s32[1,128]{1,0:T(1,128)}, u32[]{:S(2)}) copy-start(s32[1,128]{1,0:T(1,128)} %sending.1) | copy-start | bytes 1540
  0.0 66.6 %all-to-all-start = ((bf16[64,128,128]{2,1,0:T(8,128)(2,1)}), bf16[64,128,128]{2,1,0:T(8,128)(2,1)S(1)}, u32[]{:S(2)}, u32[]{:S(2)}) async-start(bf16[64,128,128]{2,1,0:T(8,128)(2,1)} %bitcast.9), calls=%async_computation | async-start | bytes 4194304 | tf_op jit(solution)/shard_map/all_to_all | solution.py:165
  18.2 1.6 %copy-start = (bf16[128,64,128]{2,1,0:T(8,128)(2,1)S(1)}, bf16[128,64,128]{2,1,0:T(8,128)(2,1)}, u32[]{:S(2)}) copy-start(bf16[128,64,128]{2,1,0:T(8,128)(2,1)} %blocks.1) | copy-start | bytes 6291460
  19.8 0.9 copy-start.3
  41.9 1.0 copy-start.1
  42.9 5.3 %collective-permute-start = (bf16[16,128,256]{2,1,0:T(8,128)(2,1)S(1)}, bf16[16,128,256]{2,1,0:T(8,128)(2,1)}, u32[]{:S(2)}, u32[]{:S(2)}) collective-permute-start(bf16[16,128,256]{2,1,0:T(8,128)(2,1)S(1)} %get-tuple-element.15), channel_id=1, source_target_pairs={{0,4},{4,0},{1,5},{5,1},{2,6},{6,2},{3,7},{7,3},{8,12},{12,8},{9,1... | collective-permute-start | bytes 3145736 | tf_op jit(solution)/shard_map/ppermute | solution.py:186

commit v5 on v4

--- a/solution.py
+++ b/solution.py
@@ -141,6 +141,11 @@
     partial[half_rows:] = jnp.where(first, pltpu.roll(real, 120, axis=1), imag)
 
 
+def fold_kernel(arrived, summed):
+    total = jnp.sum(arrived[...], axis=0)
+    summed[...] = jnp.broadcast_to(total[:, None, :], summed.shape)
+
+
 def finish_kernel(place, arrived, out):
     total = jnp.broadcast_to(jnp.sum(arrived[...], axis=0, keepdims=True), (8, 128))
     total = pltpu.roll(total, (128 - 16 * place[0]) % 128, axis=1)
@@ -166,9 +171,11 @@
         environments.reshape(plane, cores * bond, doubled), PLANE, split_axis=0, concat_axis=0, tiled=True
     )
     core = lax.axis_index("cuts_2").reshape(1).astype(jnp.int32)
-    place = lax.axis_index(NEAR).reshape(1).astype(jnp.int32)
+    place = lax.axis_index("cuts_1").reshape(1).astype(jnp.int32)
     per = bits // (near * plane)
-    owners = owner_map.reshape(2, plane // 2, near, per).transpose(1, 2, 0, 3).reshape(1, bits)
+    columns = lax.axis_size("cuts_1")
+    owners = owner_map.reshape(plane // columns, columns, near, per).transpose(2, 0, 1, 3)
+    owners = owners.reshape(2, plane // 2, columns, per).transpose(1, 2, 0, 3).reshape(1, bits)
     core, place, owners = lax.optimization_barrier((core, place, owners))
     packed_other, packed_own, left_cols = pl.pallas_call(
         advance_kernel,
@@ -208,8 +215,17 @@
         pltpu.with_memory_space_constraint(received, pltpu.HBM),
         pltpu.with_memory_space_constraint(left_cols, pltpu.HBM),
     )
-    sent = jnp.broadcast_to(partial[:, None, :], (plane, near, doubled)).reshape(plane * near, doubled)
-    arrived = lax.all_to_all(sent, CUTS_BATCH, split_axis=0, concat_axis=0, tiled=True)
+    arrived = lax.all_to_all(
+        partial.reshape(near, rows // near, doubled), NEAR, split_axis=0, concat_axis=0, tiled=True
+    )
+    summed = pl.pallas_call(
+        fold_kernel,
+        out_shape=jax.ShapeDtypeStruct((plane // columns, columns, doubled), jnp.float32),
+        in_specs=[VMEM],
+        out_specs=VMEM,
+        name="fold",
+    )(pltpu.with_memory_space_constraint(arrived, pltpu.VMEM))
+    arrived = lax.all_to_all(summed.reshape(plane, doubled), PLANE, split_axis=0, concat_axis=0, tiled=True)
     return pl.pallas_call(
         finish_kernel,
         out_shape=jax.ShapeDtypeStruct((2, per), jnp.float32),

time: 104 us -> 104 us (level)
    all_to_all x1 -> x2, blocking collectives: 33.5 us -> 32.7 us  [the longest x1 19.6 us: on_device(): lax.all_to_all(summed.reshape(plane, doubled), PLANE, split_axis=0, conca...]
where the time goes in v5:
time: 104 us; the launch traced here: 103 us
  blocking collectives  32.7 us (31%)
  Pallas kernels  25.1 us (24%)
  waiting for transfers between devices  20.5 us (20%)
  starting transfers between devices  20.1 us (19%)
  local copies, waits for them, and re-layouts  4.64 us (4%)
    pallas_call x1, Pallas kernels, on_device(): pl.pallas_call(advance_kernel, out_shape=(jax.ShapeDtypeStruct((plane //...  21.2 us
    all_to_all x1, blocking collectives, on_device(): lax.all_to_all(summed.reshape(plane, doubled), PLANE, split_axis=0, conca...  19.6 us
    all_to_all x1, waiting for transfers between devices, on_device(): lax.all_to_all(environments.reshape(plane, cores * bond, doubled), PLANE,...  18.1 us
    all_to_all x1, starting transfers between devices, on_device(): lax.all_to_all(environments.reshape(plane, cores * bond, doubled), PLANE,...  17.3 us
    all_to_all x1, blocking collectives, on_device(): lax.all_to_all(partial.reshape(near, rows // near, doubled), NEAR, split_...  13 us
    unnamed x18, local copies, waits for them, and re-layouts  3.51 us
    ppermute x1, starting transfers between devices, on_device(): received = lax.ppermute(packed_other, 'cuts_2', [(0, 1), (1, 0)])  2.86 us
    pallas_call x1, Pallas kernels, on_device(): pl.pallas_call(lambda *refs: amplitude_kernel(*refs, scale=scale), out_sh...  2.59 us
  transfers between devices with their start and end apart: 2, of which 2 were waited for; matrix products, arithmetic and copies ran while one was open for 1% of the time, Pallas kernels for 21%

profile of v5, /device:TPU:1, one launch (start us, length us, event | category | flops | bytes accessed | tf_op | source)
XLA Modules:
  0.0 103.2 jit_solution(1612677222491228033)
XLA Ops:
  0.0 0.0 copy-start.8
  0.0 0.0 copy-start.2
  0.0 0.0 copy-start.4
  0.0 0.0 copy-start.5
  0.0 0.0 copy-start.6
  0.0 0.0 copy-start.7
  0.0 17.3 %all-to-all-start = ((bf16[64,128,128]{2,1,0:T(8,128)(2,1)}), bf16[64,128,128]{2,1,0:T(8,128)(2,1)S(1)}, u32[]{:S(2)}, u32[]{:S(2)}) async-start(bf16[64,128,128]{2,1,0:T(8,128)(2,1)} %bitcast.18), calls=%async_computation | async-start | bytes 4194304 | tf_op jit(solution)/shard_map/all_to_all | solution.py:170
  17.3 0.0 copy-done.8
  17.3 0.2 reshape.30
  17.5 0.2 copy.13
  17.7 0.1 reshape.31
  17.9 0.2 copy.14
  18.1 0.4 reshape.32.owners.refs_3_
  18.5 0.0 copy-done.2
  18.5 0.0 copy-done.4
  18.5 0.0 copy-done.5
  18.5 0.0 copy-done.6
  18.5 0.0 copy-done.7
  18.6 0.0 copy-start
  18.6 1.6 %copy-done = bf16[128,64,128]{2,1,0:T(8,128)(2,1)S(1)} copy-done((bf16[128,64,128]{2,1,0:T(8,128)(2,1)S(1)}, bf16[128,64,128]{2,1,0:T(8,128)(2,1)}, u32[]{:S(2)}) %copy-start) | copy-done | bytes 2097176
  20.1 0.0 copy-start.3
  20.2 0.9 copy-done.3
  21.1 21.2 %advance.1 = (bf16[16,128,256]{2,1,0:T(8,128)(2,1)S(1)}, bf16[17,128,256]{2,1,0:T(8,128)(2,1)S(1)}, bf16[128,4096]{1,0:T(8,128)(2,1)S(1)}) custom-call(s32[1]{0:T(128)} %bitcast.core.refs_0_, s32[1,128]{1,0:T(1,128)S(1)} %copy-done.6, s32[1,128]{1,0:T(1,128)S(1)} %copy-done.7, bf16[128,64,128]{2,1,0:T(8,128)(2,1)S(1)} %copy-done, ...), custom_call_target="tpu_custom_call" | custom-call | tf_op jit(solution)/shard_map/advance/pallas_call | solution.py:180
  42.3 0.0 copy-start.1
  42.3 1.0 copy-done.1
  43.3 2.9 %collective-permute-start = (bf16[16,128,256]{2,1,0:T(8,128)(2,1)S(1)}, bf16[16,128,256]{2,1,0:T(8,128)(2,1)}, u32[]{:S(2)}, u32[]{:S(2)}) collective-permute-start(bf16[16,128,256]{2,1,0:T(8,128)(2,1)S(1)} %get-tuple-element.15), channel_id=1, source_target_pairs={{0,4},{4,0},{1,5},{5,1},{2,6},{6,2},{3,7},{7,3},{8,12},{12,8},{9,1... | collective-permute-start | bytes 3145736 | tf_op jit(solution)/shard_map/ppermute | solution.py:193
  46.1 2.4 %collective-permute-done.refs_4_ = bf16[16,128,256]{2,1,0:T(8,128)(2,1)} collective-permute-done((bf16[16,128,256]{2,1,0:T(8,128)(2,1)S(1)}, bf16[16,128,256]{2,1,0:T(8,128)(2,1)}, u32[]{:S(2)}, u32[]{:S(2)}) %collective-permute-start) | collective-permute-done | bytes 1048608 | tf_op jit(solution)/shard_map/ppermute | solution.py:193
  48.5 18.1 %all-to-all-done = bf16[64,128,128]{2,1,0:T(8,128)(2,1)S(1)} async-done(((bf16[64,128,128]{2,1,0:T(8,128)(2,1)}), bf16[64,128,128]{2,1,0:T(8,128)(2,1)S(1)}, u32[]{:S(2)}, u32[]{:S(2)}) %all-to-all-start) | async-done | bytes 2097184 | tf_op jit(solution)/shard_map/all_to_all | solution.py:170
  66.6 2.6 %amplitudes.1 = f32[64,128]{1,0:T(8,128)S(1)} custom-call(s32[1]{0:T(128)} %bitcast.core.refs_0_, bf16[17,128,256]{2,1,0:T(8,128)(2,1)S(1)} %get-tuple-element.14.refs_1_, bf16[64,2,64,128]{3,2,1,0:T(8,128)(2,1)S(1)} %bitcast.15, s32[1,4096]{1,0:T(1,128)S(1)} %reshape.32.owners.refs_3_, bf16[16,128,256]{2,1,0:T(8,128)(2,1)} %collective-permute-done.refs_4_, ...), custom_call_target="tpu_custom_call" | custom-call | tf_op jit(solution)/shard_map/amplitudes/pallas_call | solution.py:196
  69.2 13.0 %all_to_all.21.arrived = f32[8,8,128]{2,1,0:T(8,128)S(1)} all-to-all(f32[8,8,128]{2,1,0:T(8,128)S(1)} %bitcast.16), channel_id=1, replica_groups=mesh['cuts_0'=8,'cuts_1'=8,'cuts_2'=2,'batch'=4] {'cuts_2','batch'}, dimensions={0} | all-to-all | bytes 65536 | tf_op jit(solution)/shard_map/all_to_all | solution.py:218
  82.3 0.6 fold.1
  82.9 19.6 %all_to_all.22 = f32[64,1,128]{2,1,0:T(1,128)S(1)} all-to-all(f32[64,1,128]{2,1,0:T(1,128)} %bitcast.21), channel_id=1, replica_groups=mesh['cuts_0'=8,'cuts_1'=8,'cuts_2'=2,'batch'=4] {'cuts_0','cuts_1'}, dimensions={0} | all-to-all | bytes 65536 | tf_op jit(solution)/shard_map/all_to_all | solution.py:228
  102.5 0.7 finish.1
Async XLA Ops:
  0.0 17.3 %copy-start.8 = (s32[4096]{0:T(1024)S(1)}, s32[4096]{0:T(1024)}, u32[]{:S(2)}) copy-start(s32[4096]{0:T(1024)} %param.17) | copy-start | bytes 49156
  0.0 18.5 %copy-start.2 = (bf16[128,8,128]{2,1,0:T(8,128)(2,1)S(1)}, bf16[128,8,128]{2,1,0:T(8,128)(2,1)}, u32[]{:S(2)}) copy-start(bf16[128,8,128]{2,1,0:T(8,128)(2,1)} %selectors.1) | copy-start | bytes 786436
  0.0 18.5 %copy-start.4 = (bf16[64,128]{1,0:T(8,128)(2,1)S(1)}, bf16[64,128]{1,0:T(8,128)(2,1)}, u32[]{:S(2)}) copy-start(bf16[64,128]{1,0:T(8,128)(2,1)} %left.1) | copy-start | bytes 49156
  0.0 18.5 %copy-start.5 = (bf16[64,128]{1,0:T(8,128)(2,1)S(1)}, bf16[64,128]{1,0:T(8,128)(2,1)}, u32[]{:S(2)}) copy-start(bf16[64,128]{1,0:T(8,128)(2,1)} %right.1) | copy-start | bytes 49156
  0.0 18.5 %copy-start.6 = (s32[1,128]{1,0:T(1,128)S(1)}, s32[1,128]{1,0:T(1,128)}, u32[]{:S(2)}) copy-start(s32[1,128]{1,0:T(1,128)} %levels.1) | copy-start | bytes 1540
  0.0 18.5 %copy-start.7 = (s32[1,128]{1,0:T(1,128)S(1)}, s32[1,128]{1,0:T(1,128)}, u32[]{:S(2)}) copy-start(s32[1,128]{1,0:T(1,128)} %sending.1) | copy-start | bytes 1540
  0.0 66.6 %all-to-all-start = ((bf16[64,128,128]{2,1,0:T(8,128)(2,1)}), bf16[64,128,128]{2,1,0:T(8,128)(2,1)S(1)}, u32[]{:S(2)}, u32[]{:S(2)}) async-start(bf16[64,128,128]{2,1,0:T(8,128)(2,1)} %bitcast.18), calls=%async_computation | async-start | bytes 4194304 | tf_op jit(solution)/shard_map/all_to_all | solution.py:170
  18.6 1.6 %copy-start = (bf16[128,64,128]{2,1,0:T(8,128)(2,1)S(1)}, bf16[128,64,128]{2,1,0:T(8,128)(2,1)}, u32[]{:S(2)}) copy-start(bf16[128,64,128]{2,1,0:T(8,128)(2,1)} %blocks.1) | copy-start | bytes 6291460
  20.1 0.9 copy-start.3
  42.3 1.0 copy-start.1
  43.3 5.3 %collective-permute-start = (bf16[16,128,256]{2,1,0:T(8,128)(2,1)S(1)}, bf16[16,128,256]{2,1,0:T(8,128)(2,1)}, u32[]{:S(2)}, u32[]{:S(2)}) collective-permute-start(bf16[16,128,256]{2,1,0:T(8,128)(2,1)S(1)} %get-tuple-element.15), channel_id=1, source_target_pairs={{0,4},{4,0},{1,5},{5,1},{2,6},{6,2},{3,7},{7,3},{8,12},{12,8},{9,1... | collective-permute-start | bytes 3145736 | tf_op jit(solution)/shard_map/ppermute | solution.py:193

commit v6 on v5

--- a/solution.py
+++ b/solution.py
@@ -174,7 +174,9 @@
     place = lax.axis_index("cuts_1").reshape(1).astype(jnp.int32)
     per = bits // (near * plane)
     columns = lax.axis_size("cuts_1")
-    owners = owner_map.reshape(plane // columns, columns, near, per).transpose(2, 0, 1, 3)
+    half = plane // columns // 2
+    owners = owner_map.reshape(2, half * columns * near * per)[::-1]
+    owners = owners.reshape(plane // columns, columns, near, per).transpose(2, 0, 1, 3)
     owners = owners.reshape(2, plane // 2, columns, per).transpose(1, 2, 0, 3).reshape(1, bits)
     core, place, owners = lax.optimization_barrier((core, place, owners))
     packed_other, packed_own, left_cols = pl.pallas_call(
@@ -225,7 +227,19 @@
         out_specs=VMEM,
         name="fold",
     )(pltpu.with_memory_space_constraint(arrived, pltpu.VMEM))
-    arrived = lax.all_to_all(summed.reshape(plane, doubled), PLANE, split_axis=0, concat_axis=0, tiled=True)
+    far_first = [
+        (row + half) % (2 * half) * columns + (column + columns // 2) % columns
+        for row in range(2 * half)
+        for column in range(columns)
+    ]
+    arrived = lax.all_to_all(
+        summed.reshape(plane, doubled),
+        PLANE,
+        split_axis=0,
+        concat_axis=0,
+        tiled=True,
+        axis_index_groups=[far_first],
+    )
     return pl.pallas_call(
         finish_kernel,
         out_shape=jax.ShapeDtypeStruct((2, per), jnp.float32),

time: 104 us -> 98.5 us (0.947)
  blocking collectives: 32.7 us -> 27.4 us
    all_to_all x1, blocking collectives: 19.6 us -> 14.3 us  [on_device(): lax.all_to_all(summed.reshape(plane, doubled), PLANE, split_axis=0, conca...]
  transfers between devices with their start and end apart: 2 -> 2, of which waited for: 2 -> 2; matrix products, arithmetic and copies ran while one was open for 1% -> 2% of each run, Pallas kernels for 21% -> 22%
where the time goes in v6:
time: 98.5 us; the launch traced here: 97.9 us
  blocking collectives  27.4 us (28%)
  Pallas kernels  25.1 us (25%)
  starting transfers between devices  20.1 us (20%)
  waiting for transfers between devices  20 us (20%)
  local copies, waits for them, and re-layouts  5.08 us (5%)
    pallas_call x1, Pallas kernels, on_device(): pl.pallas_call(advance_kernel, out_shape=(jax.ShapeDtypeStruct((plane //...  21.2 us
    all_to_all x1, waiting for transfers between devices, on_device(): lax.all_to_all(environments.reshape(plane, cores * bond, doubled), PLANE,...  17.6 us
    all_to_all x1, starting transfers between devices, on_device(): lax.all_to_all(environments.reshape(plane, cores * bond, doubled), PLANE,...  17.3 us
    all_to_all x1, blocking collectives, on_device(): lax.all_to_all(summed.reshape(plane, doubled), PLANE, split_axis=0, conca...  14.3 us
    all_to_all x1, blocking collectives, on_device(): lax.all_to_all(partial.reshape(near, rows // near, doubled), NEAR, split_...  13 us
    unnamed x18, local copies, waits for them, and re-layouts  3.51 us
    ppermute x1, starting transfers between devices, on_device(): received = lax.ppermute(packed_other, 'cuts_2', [(0, 1), (1, 0)])  2.87 us
    pallas_call x1, Pallas kernels, on_device(): pl.pallas_call(lambda *refs: amplitude_kernel(*refs, scale=scale), out_sh...  2.59 us
  transfers between devices with their start and end apart: 2, of which 2 were waited for; matrix products, arithmetic and copies ran while one was open for 2% of the time, Pallas kernels for 22%

profile of v6, /device:TPU:1, one launch (start us, length us, event | category | flops | bytes accessed | tf_op | source)
XLA Modules:
  0.0 97.9 jit_solution(13572306647559606041)
XLA Ops:
  0.0 0.0 copy-start.8
  0.0 0.0 copy-start.2
  0.0 0.0 copy-start.4
  0.0 0.0 copy-start.5
  0.0 0.0 copy-start.6
  0.0 0.0 copy-start.7
  0.0 17.3 %all-to-all-start = ((bf16[64,128,128]{2,1,0:T(8,128)(2,1)}), bf16[64,128,128]{2,1,0:T(8,128)(2,1)S(1)}, u32[]{:S(2)}, u32[]{:S(2)}) async-start(bf16[64,128,128]{2,1,0:T(8,128)(2,1)} %bitcast.18), calls=%async_computation | async-start | bytes 4194304 | tf_op jit(solution)/shard_map/all_to_all | solution.py:170
  17.3 0.0 copy-done.8
  17.4 0.4 rev.3
  17.8 0.2 reshape.34
  18.0 0.2 copy.13
  18.2 0.1 reshape.35
  18.3 0.2 copy.14
  18.6 0.4 reshape.36.owners.refs_3_
  19.0 0.0 copy-done.2
  19.0 0.0 copy-done.4
  19.0 0.0 copy-done.5
  19.0 0.0 copy-done.6
  19.0 0.0 copy-done.7
  19.0 0.0 copy-start
  19.0 1.6 %copy-done = bf16[128,64,128]{2,1,0:T(8,128)(2,1)S(1)} copy-done((bf16[128,64,128]{2,1,0:T(8,128)(2,1)S(1)}, bf16[128,64,128]{2,1,0:T(8,128)(2,1)}, u32[]{:S(2)}) %copy-start) | copy-done | bytes 2097176
  20.6 0.0 copy-start.3
  20.6 0.9 copy-done.3
  21.5 21.2 %advance.1 = (bf16[16,128,256]{2,1,0:T(8,128)(2,1)S(1)}, bf16[17,128,256]{2,1,0:T(8,128)(2,1)S(1)}, bf16[128,4096]{1,0:T(8,128)(2,1)S(1)}) custom-call(s32[1]{0:T(128)} %bitcast.core.refs_0_, s32[1,128]{1,0:T(1,128)S(1)} %copy-done.6, s32[1,128]{1,0:T(1,128)S(1)} %copy-done.7, bf16[128,64,128]{2,1,0:T(8,128)(2,1)S(1)} %copy-done, ...), custom_call_target="tpu_custom_call" | custom-call | tf_op jit(solution)/shard_map/advance/pallas_call | solution.py:182
  42.7 0.0 copy-start.1
  42.7 1.0 %copy-done.1 = bf16[128,4096]{1,0:T(8,128)(2,1)} copy-done((bf16[128,4096]{1,0:T(8,128)(2,1)}, bf16[128,4096]{1,0:T(8,128)(2,1)S(1)}, u32[]{:S(2)}) %copy-start.1) | copy-done | bytes 1048600
  43.7 2.9 %collective-permute-start = (bf16[16,128,256]{2,1,0:T(8,128)(2,1)S(1)}, bf16[16,128,256]{2,1,0:T(8,128)(2,1)}, u32[]{:S(2)}, u32[]{:S(2)}) collective-permute-start(bf16[16,128,256]{2,1,0:T(8,128)(2,1)S(1)} %get-tuple-element.15), channel_id=1, source_target_pairs={{0,4},{4,0},{1,5},{5,1},{2,6},{6,2},{3,7},{7,3},{8,12},{12,8},{9,1... | collective-permute-start | bytes 3145736 | tf_op jit(solution)/shard_map/ppermute | solution.py:195
  46.6 2.4 %collective-permute-done.refs_4_ = bf16[16,128,256]{2,1,0:T(8,128)(2,1)} collective-permute-done((bf16[16,128,256]{2,1,0:T(8,128)(2,1)S(1)}, bf16[16,128,256]{2,1,0:T(8,128)(2,1)}, u32[]{:S(2)}, u32[]{:S(2)}) %collective-permute-start) | collective-permute-done | bytes 1048608 | tf_op jit(solution)/shard_map/ppermute | solution.py:195
  49.0 17.6 %all-to-all-done = bf16[64,128,128]{2,1,0:T(8,128)(2,1)S(1)} async-done(((bf16[64,128,128]{2,1,0:T(8,128)(2,1)}), bf16[64,128,128]{2,1,0:T(8,128)(2,1)S(1)}, u32[]{:S(2)}, u32[]{:S(2)}) %all-to-all-start) | async-done | bytes 2097184 | tf_op jit(solution)/shard_map/all_to_all | solution.py:170
  66.6 2.6 %amplitudes.1 = f32[64,128]{1,0:T(8,128)S(1)} custom-call(s32[1]{0:T(128)} %bitcast.core.refs_0_, bf16[17,128,256]{2,1,0:T(8,128)(2,1)S(1)} %get-tuple-element.14.refs_1_, bf16[64,2,64,128]{3,2,1,0:T(8,128)(2,1)S(1)} %bitcast.15, s32[1,4096]{1,0:T(1,128)S(1)} %reshape.36.owners.refs_3_, bf16[16,128,256]{2,1,0:T(8,128)(2,1)} %collective-permute-done.refs_4_, ...), custom_call_target="tpu_custom_call" | custom-call | tf_op jit(solution)/shard_map/amplitudes/pallas_call | solution.py:198
  69.2 13.0 %all_to_all.21.arrived = f32[8,8,128]{2,1,0:T(8,128)S(1)} all-to-all(f32[8,8,128]{2,1,0:T(8,128)S(1)} %bitcast.16), channel_id=1, replica_groups=mesh['cuts_0'=8,'cuts_1'=8,'cuts_2'=2,'batch'=4] {'cuts_2','batch'}, dimensions={0} | all-to-all | bytes 65536 | tf_op jit(solution)/shard_map/all_to_all | solution.py:220
  82.3 0.6 fold.1
  82.9 14.3 %all_to_all.22 = f32[64,1,128]{2,1,0:T(1,128)S(1)} all-to-all(f32[64,1,128]{2,1,0:T(1,128)} %bitcast.21), channel_id=1, replica_groups={{288,296,304,312,256,264,272,280,352,360,368,376,320,328,336,344,416,42..., dimensions={0} | all-to-all | bytes 65536 | tf_op jit(solution)/shard_map/all_to_all | solution.py:235
  97.2 0.7 finish.1
  (1 shorter events, 0.0 us)
Async XLA Ops:
  0.0 17.3 %copy-start.8 = (s32[4096]{0:T(1024)S(1)}, s32[4096]{0:T(1024)}, u32[]{:S(2)}) copy-start(s32[4096]{0:T(1024)} %param.17) | copy-start | bytes 49156
  0.0 19.0 %copy-start.2 = (bf16[128,8,128]{2,1,0:T(8,128)(2,1)S(1)}, bf16[128,8,128]{2,1,0:T(8,128)(2,1)}, u32[]{:S(2)}) copy-start(bf16[128,8,128]{2,1,0:T(8,128)(2,1)} %selectors.1) | copy-start | bytes 786436
  0.0 19.0 %copy-start.4 = (bf16[64,128]{1,0:T(8,128)(2,1)S(1)}, bf16[64,128]{1,0:T(8,128)(2,1)}, u32[]{:S(2)}) copy-start(bf16[64,128]{1,0:T(8,128)(2,1)} %left.1) | copy-start | bytes 49156
  0.0 19.0 %copy-start.5 = (bf16[64,128]{1,0:T(8,128)(2,1)S(1)}, bf16[64,128]{1,0:T(8,128)(2,1)}, u32[]{:S(2)}) copy-start(bf16[64,128]{1,0:T(8,128)(2,1)} %right.1) | copy-start | bytes 49156
  0.0 19.0 %copy-start.6 = (s32[1,128]{1,0:T(1,128)S(1)}, s32[1,128]{1,0:T(1,128)}, u32[]{:S(2)}) copy-start(s32[1,128]{1,0:T(1,128)} %levels.1) | copy-start | bytes 1540
  0.0 19.0 %copy-start.7 = (s32[1,128]{1,0:T(1,128)S(1)}, s32[1,128]{1,0:T(1,128)}, u32[]{:S(2)}) copy-start(s32[1,128]{1,0:T(1,128)} %sending.1) | copy-start | bytes 1540
  0.0 66.6 %all-to-all-start = ((bf16[64,128,128]{2,1,0:T(8,128)(2,1)}), bf16[64,128,128]{2,1,0:T(8,128)(2,1)S(1)}, u32[]{:S(2)}, u32[]{:S(2)}) async-start(bf16[64,128,128]{2,1,0:T(8,128)(2,1)} %bitcast.18), calls=%async_computation | async-start | bytes 4194304 | tf_op jit(solution)/shard_map/all_to_all | solution.py:170
  19.0 1.6 %copy-start = (bf16[128,64,128]{2,1,0:T(8,128)(2,1)S(1)}, bf16[128,64,128]{2,1,0:T(8,128)(2,1)}, u32[]{:S(2)}) copy-start(bf16[128,64,128]{2,1,0:T(8,128)(2,1)} %blocks.1) | copy-start | bytes 6291460
  20.6 0.9 copy-start.3
  42.7 1.0 %copy-start.1 = (bf16[128,4096]{1,0:T(8,128)(2,1)}, bf16[128,4096]{1,0:T(8,128)(2,1)S(1)}, u32[]{:S(2)}) copy-start(bf16[128,4096]{1,0:T(8,128)(2,1)S(1)} %get-tuple-element.16.refs_5_) | copy-start | bytes 3145732
  43.7 5.3 %collective-permute-start = (bf16[16,128,256]{2,1,0:T(8,128)(2,1)S(1)}, bf16[16,128,256]{2,1,0:T(8,128)(2,1)}, u32[]{:S(2)}, u32[]{:S(2)}) collective-permute-start(bf16[16,128,256]{2,1,0:T(8,128)(2,1)S(1)} %get-tuple-element.15), channel_id=1, source_target_pairs={{0,4},{4,0},{1,5},{5,1},{2,6},{6,2},{3,7},{7,3},{8,12},{12,8},{9,1... | collective-permute-start | bytes 3145736 | tf_op jit(solution)/shard_map/ppermute | solution.py:195

commit v7 on v6

--- a/solution.py
+++ b/solution.py
@@ -176,6 +176,7 @@
     columns = lax.axis_size("cuts_1")
     half = plane // columns // 2
     owners = owner_map.reshape(2, half * columns * near * per)[::-1]
+    owners = owners.reshape(plane, 2 * cores, near // cores // 2 * per)[:, ::-1]
     owners = owners.reshape(plane // columns, columns, near, per).transpose(2, 0, 1, 3)
     owners = owners.reshape(2, plane // 2, columns, per).transpose(1, 2, 0, 3).reshape(1, bits)
     core, place, owners = lax.optimization_barrier((core, place, owners))
@@ -217,8 +218,17 @@
         pltpu.with_memory_space_constraint(received, pltpu.HBM),
         pltpu.with_memory_space_constraint(left_cols, pltpu.HBM),
     )
+    across = near // cores
+    near_first = [
+        (cores - 1 - side) * across + (step + across // 2) % across for side in range(cores) for step in range(across)
+    ]
     arrived = lax.all_to_all(
-        partial.reshape(near, rows // near, doubled), NEAR, split_axis=0, concat_axis=0, tiled=True
+        partial.reshape(near, rows // near, doubled),
+        NEAR,
+        split_axis=0,
+        concat_axis=0,
+        tiled=True,
+        axis_index_groups=[near_first],
     )
     summed = pl.pallas_call(
         fold_kernel,

time: 98.5 us -> 96.7 us (0.982)
  blocking collectives: 27.4 us -> 25.2 us
    all_to_all x1, blocking collectives: 13 us -> 10.9 us  [on_device(): lax.all_to_all(partial.reshape(near, rows // near, doubled), NEAR, split_...]
where the time goes in v7:
time: 96.7 us; the launch traced here: 95.7 us
  blocking collectives  25.2 us (26%)
  Pallas kernels  25.1 us (26%)
  starting transfers between devices  20.1 us (21%)
  waiting for transfers between devices  19.6 us (20%)
  local copies, waits for them, and re-layouts  5.49 us (6%)
    pallas_call x1, Pallas kernels, on_device(): pl.pallas_call(advance_kernel, out_shape=(jax.ShapeDtypeStruct((plane //...  21.2 us
    all_to_all x1, starting transfers between devices, on_device(): lax.all_to_all(environments.reshape(plane, cores * bond, doubled), PLANE,...  17.3 us
    all_to_all x1, waiting for transfers between devices, on_device(): lax.all_to_all(environments.reshape(plane, cores * bond, doubled), PLANE,...  17.2 us
    all_to_all x1, blocking collectives, on_device(): lax.all_to_all(summed.reshape(plane, doubled), PLANE, split_axis=0, conca...  14.3 us
    all_to_all x1, blocking collectives, on_device(): lax.all_to_all(partial.reshape(near, rows // near, doubled), NEAR, split_...  10.9 us
    unnamed x18, local copies, waits for them, and re-layouts  3.52 us
    ppermute x1, starting transfers between devices, on_device(): received = lax.ppermute(packed_other, 'cuts_2', [(0, 1), (1, 0)])  2.85 us
    pallas_call x1, Pallas kernels, on_device(): pl.pallas_call(lambda *refs: amplitude_kernel(*refs, scale=scale), out_sh...  2.59 us
  transfers between devices with their start and end apart: 2, of which 2 were waited for; matrix products, arithmetic and copies ran while one was open for 2% of the time, Pallas kernels for 22%

profile of v7, /device:TPU:1, one launch (start us, length us, event | category | flops | bytes accessed | tf_op | source)
XLA Modules:
  0.0 95.7 jit_solution(18229825838585029012)
XLA Ops:
  0.0 0.0 copy-start.8
  0.0 17.3 %all-to-all-start = ((bf16[64,128,128]{2,1,0:T(8,128)(2,1)}), bf16[64,128,128]{2,1,0:T(8,128)(2,1)S(1)}, u32[]{:S(2)}, u32[]{:S(2)}) async-start(bf16[64,128,128]{2,1,0:T(8,128)(2,1)} %bitcast.20), calls=%async_computation | async-start | bytes 4194304 | tf_op jit(solution)/shard_map/all_to_all | solution.py:170
  17.3 0.0 copy-start.2
  17.3 0.0 copy-start.4
  17.3 0.0 copy-start.5
  17.3 0.0 copy-start.6
  17.3 0.0 copy-start.7
  17.3 0.0 copy-done.8
  17.4 0.4 rev.6
  17.8 0.1 reshape.37
  17.9 0.2 rev.7
  18.1 0.1 copy.13
  18.2 0.1 reshape.38
  18.3 0.3 copy.14
  18.6 0.1 reshape.39
  18.7 0.2 copy.15
  19.0 0.4 reshape.40.owners.refs_3_
  19.4 0.0 copy-done.2
  19.4 0.0 copy-done.4
  19.4 0.0 copy-done.5
  19.4 0.0 copy-done.6
  19.4 0.0 copy-done.7
  19.4 0.0 copy-start
  19.4 1.6 %copy-done = bf16[128,64,128]{2,1,0:T(8,128)(2,1)S(1)} copy-done((bf16[128,64,128]{2,1,0:T(8,128)(2,1)S(1)}, bf16[128,64,128]{2,1,0:T(8,128)(2,1)}, u32[]{:S(2)}) %copy-start) | copy-done | bytes 2097176
  21.0 0.0 copy-start.3
  21.0 0.9 copy-done.3
  21.9 21.2 %advance.1 = (bf16[16,128,256]{2,1,0:T(8,128)(2,1)S(1)}, bf16[17,128,256]{2,1,0:T(8,128)(2,1)S(1)}, bf16[128,4096]{1,0:T(8,128)(2,1)S(1)}) custom-call(s32[1]{0:T(128)} %bitcast.core.refs_0_, s32[1,128]{1,0:T(1,128)S(1)} %copy-done.6, s32[1,128]{1,0:T(1,128)S(1)} %copy-done.7, bf16[128,64,128]{2,1,0:T(8,128)(2,1)S(1)} %copy-done, ...), custom_call_target="tpu_custom_call" | custom-call | tf_op jit(solution)/shard_map/advance/pallas_call | solution.py:183
  43.2 0.0 copy-start.1
  43.2 1.0 %copy-done.1 = bf16[128,4096]{1,0:T(8,128)(2,1)} copy-done((bf16[128,4096]{1,0:T(8,128)(2,1)}, bf16[128,4096]{1,0:T(8,128)(2,1)S(1)}, u32[]{:S(2)}) %copy-start.1) | copy-done | bytes 1048600
  44.2 2.9 %collective-permute-start = (bf16[16,128,256]{2,1,0:T(8,128)(2,1)S(1)}, bf16[16,128,256]{2,1,0:T(8,128)(2,1)}, u32[]{:S(2)}, u32[]{:S(2)}) collective-permute-start(bf16[16,128,256]{2,1,0:T(8,128)(2,1)S(1)} %get-tuple-element.15), channel_id=1, source_target_pairs={{0,4},{4,0},{1,5},{5,1},{2,6},{6,2},{3,7},{7,3},{8,12},{12,8},{9,1... | collective-permute-start | bytes 3145736 | tf_op jit(solution)/shard_map/ppermute | solution.py:196
  47.0 2.4 %collective-permute-done.refs_4_ = bf16[16,128,256]{2,1,0:T(8,128)(2,1)} collective-permute-done((bf16[16,128,256]{2,1,0:T(8,128)(2,1)S(1)}, bf16[16,128,256]{2,1,0:T(8,128)(2,1)}, u32[]{:S(2)}, u32[]{:S(2)}) %collective-permute-start) | collective-permute-done | bytes 1048608 | tf_op jit(solution)/shard_map/ppermute | solution.py:196
  49.4 17.2 %all-to-all-done = bf16[64,128,128]{2,1,0:T(8,128)(2,1)S(1)} async-done(((bf16[64,128,128]{2,1,0:T(8,128)(2,1)}), bf16[64,128,128]{2,1,0:T(8,128)(2,1)S(1)}, u32[]{:S(2)}, u32[]{:S(2)}) %all-to-all-start) | async-done | bytes 2097184 | tf_op jit(solution)/shard_map/all_to_all | solution.py:170
  66.6 2.6 %amplitudes.1 = f32[64,128]{1,0:T(8,128)S(1)} custom-call(s32[1]{0:T(128)} %bitcast.core.refs_0_, bf16[17,128,256]{2,1,0:T(8,128)(2,1)S(1)} %get-tuple-element.14.refs_1_, bf16[64,2,64,128]{3,2,1,0:T(8,128)(2,1)S(1)} %bitcast.17, s32[1,4096]{1,0:T(1,128)S(1)} %reshape.40.owners.refs_3_, bf16[16,128,256]{2,1,0:T(8,128)(2,1)} %collective-permute-done.refs_4_, ...), custom_call_target="tpu_custom_call" | custom-call | tf_op jit(solution)/shard_map/amplitudes/pallas_call | solution.py:199
  69.2 10.9 %all_to_all.21.arrived = f32[8,8,128]{2,1,0:T(8,128)S(1)} all-to-all(f32[8,8,128]{2,1,0:T(8,128)S(1)} %bitcast.18), channel_id=1, replica_groups={{6,7,4,5,2,3,0,1},{14,15,12,13,10,11,8,9},{22,23,20,21,18,19,16,17},{30..., dimensions={0} | all-to-all | bytes 65536 | tf_op jit(solution)/shard_map/all_to_all | solution.py:225
  80.1 0.6 fold.1
  80.7 14.3 %all_to_all.22 = f32[64,1,128]{2,1,0:T(1,128)S(1)} all-to-all(f32[64,1,128]{2,1,0:T(1,128)} %bitcast.23), channel_id=1, replica_groups={{288,296,304,312,256,264,272,280,352,360,368,376,320,328,336,344,416,42..., dimensions={0} | all-to-all | bytes 65536 | tf_op jit(solution)/shard_map/all_to_all | solution.py:245
  95.0 0.7 finish.1
  (1 shorter events, 0.0 us)
Async XLA Ops:
  0.0 17.3 %copy-start.8 = (s32[4096]{0:T(1024)S(1)}, s32[4096]{0:T(1024)}, u32[]{:S(2)}) copy-start(s32[4096]{0:T(1024)} %param.17) | copy-start | bytes 49156
  0.0 66.6 %all-to-all-start = ((bf16[64,128,128]{2,1,0:T(8,128)(2,1)}), bf16[64,128,128]{2,1,0:T(8,128)(2,1)S(1)}, u32[]{:S(2)}, u32[]{:S(2)}) async-start(bf16[64,128,128]{2,1,0:T(8,128)(2,1)} %bitcast.20), calls=%async_computation | async-start | bytes 4194304 | tf_op jit(solution)/shard_map/all_to_all | solution.py:170
  17.3 2.1 %copy-start.2 = (bf16[128,8,128]{2,1,0:T(8,128)(2,1)S(1)}, bf16[128,8,128]{2,1,0:T(8,128)(2,1)}, u32[]{:S(2)}) copy-start(bf16[128,8,128]{2,1,0:T(8,128)(2,1)} %selectors.1) | copy-start | bytes 786436
  17.3 2.1 %copy-start.4 = (bf16[64,128]{1,0:T(8,128)(2,1)S(1)}, bf16[64,128]{1,0:T(8,128)(2,1)}, u32[]{:S(2)}) copy-start(bf16[64,128]{1,0:T(8,128)(2,1)} %left.1) | copy-start | bytes 49156
  17.3 2.1 %copy-start.5 = (bf16[64,128]{1,0:T(8,128)(2,1)S(1)}, bf16[64,128]{1,0:T(8,128)(2,1)}, u32[]{:S(2)}) copy-start(bf16[64,128]{1,0:T(8,128)(2,1)} %right.1) | copy-start | bytes 49156
  17.3 2.1 %copy-start.6 = (s32[1,128]{1,0:T(1,128)S(1)}, s32[1,128]{1,0:T(1,128)}, u32[]{:S(2)}) copy-start(s32[1,128]{1,0:T(1,128)} %levels.1) | copy-start | bytes 1540
  17.3 2.1 %copy-start.7 = (s32[1,128]{1,0:T(1,128)S(1)}, s32[1,128]{1,0:T(1,128)}, u32[]{:S(2)}) copy-start(s32[1,128]{1,0:T(1,128)} %sending.1) | copy-start | bytes 1540
  19.4 1.6 %copy-start = (bf16[128,64,128]{2,1,0:T(8,128)(2,1)S(1)}, bf16[128,64,128]{2,1,0:T(8,128)(2,1)}, u32[]{:S(2)}) copy-start(bf16[128,64,128]{2,1,0:T(8,128)(2,1)} %blocks.1) | copy-start | bytes 6291460
  21.0 0.9 copy-start.3
  43.2 1.0 %copy-start.1 = (bf16[128,4096]{1,0:T(8,128)(2,1)}, bf16[128,4096]{1,0:T(8,128)(2,1)S(1)}, u32[]{:S(2)}) copy-start(bf16[128,4096]{1,0:T(8,128)(2,1)S(1)} %get-tuple-element.16.refs_5_) | copy-start | bytes 3145732
  44.2 5.3 %collective-permute-start = (bf16[16,128,256]{2,1,0:T(8,128)(2,1)S(1)}, bf16[16,128,256]{2,1,0:T(8,128)(2,1)}, u32[]{:S(2)}, u32[]{:S(2)}) collective-permute-start(bf16[16,128,256]{2,1,0:T(8,128)(2,1)S(1)} %get-tuple-element.15), channel_id=1, source_target_pairs={{0,4},{4,0},{1,5},{5,1},{2,6},{6,2},{3,7},{7,3},{8,12},{12,8},{9,1... | collective-permute-start | bytes 3145736 | tf_op jit(solution)/shard_map/ppermute | solution.py:196

commit v8 on v7

--- a/solution.py
+++ b/solution.py
@@ -11,7 +11,7 @@
 PLANE = ("cuts_0", "cuts_1")
 NEAR = ("cuts_2", "batch")
 TOGETHER = 8
-PARTS = 4
+PARTS = 2
 
 
 def lower_half(shape):

time: 96.7 us -> 96.7 us (level)
  no operation moved by 1% of the time
where the time goes in v8:
time: 96.7 us; the launch traced here: 95.7 us
  Pallas kernels  25.2 us (26%)
  blocking collectives  25.2 us (26%)
  starting transfers between devices  20.1 us (21%)
  waiting for transfers between devices  19.6 us (20%)
  local copies, waits for them, and re-layouts  5.49 us (6%)
    pallas_call x1, Pallas kernels, on_device(): pl.pallas_call(advance_kernel, out_shape=(jax.ShapeDtypeStruct((plane //...  21.2 us
    all_to_all x1, starting transfers between devices, on_device(): lax.all_to_all(environments.reshape(plane, cores * bond, doubled), PLANE,...  17.3 us
    all_to_all x1, waiting for transfers between devices, on_device(): lax.all_to_all(environments.reshape(plane, cores * bond, doubled), PLANE,...  17.2 us
    all_to_all x1, blocking collectives, on_device(): lax.all_to_all(summed.reshape(plane, doubled), PLANE, split_axis=0, conca...  14.3 us
    all_to_all x1, blocking collectives, on_device(): lax.all_to_all(partial.reshape(near, rows // near, doubled), NEAR, split_...  10.9 us
    unnamed x18, local copies, waits for them, and re-layouts  3.52 us
    ppermute x1, starting transfers between devices, on_device(): received = lax.ppermute(packed_other, 'cuts_2', [(0, 1), (1, 0)])  2.83 us
    pallas_call x1, Pallas kernels, on_device(): pl.pallas_call(lambda *refs: amplitude_kernel(*refs, scale=scale), out_sh...  2.6 us
  transfers between devices with their start and end apart: 2, of which 2 were waited for; matrix products, arithmetic and copies ran while one was open for 2% of the time, Pallas kernels for 22%

profile of v8, /device:TPU:1, one launch (start us, length us, event | category | flops | bytes accessed | tf_op | source)
XLA Modules:
  0.0 95.7 jit_solution(8920858117673922204)
XLA Ops:
  0.0 0.0 copy-start.8
  0.0 17.3 %all-to-all-start = ((bf16[64,128,128]{2,1,0:T(8,128)(2,1)}), bf16[64,128,128]{2,1,0:T(8,128)(2,1)S(1)}, u32[]{:S(2)}, u32[]{:S(2)}) async-start(bf16[64,128,128]{2,1,0:T(8,128)(2,1)} %bitcast.20), calls=%async_computation | async-start | bytes 4194304 | tf_op jit(solution)/shard_map/all_to_all | solution.py:170
  17.3 0.0 copy-start.2
  17.3 0.0 copy-start.4
  17.3 0.0 copy-start.5
  17.3 0.0 copy-start.6
  17.3 0.0 copy-start.7
  17.3 0.0 copy-done.8
  17.4 0.4 rev.6
  17.8 0.1 reshape.37
  17.9 0.2 rev.7
  18.1 0.1 copy.13
  18.2 0.1 reshape.38
  18.3 0.3 copy.14
  18.6 0.1 reshape.39
  18.7 0.2 copy.15
  19.0 0.4 reshape.40.owners.refs_3_
  19.4 0.0 copy-done.2
  19.4 0.0 copy-done.4
  19.4 0.0 copy-done.5
  19.4 0.0 copy-done.6
  19.4 0.0 copy-done.7
  19.4 0.0 copy-start
  19.4 1.6 %copy-done = bf16[128,64,128]{2,1,0:T(8,128)(2,1)S(1)} copy-done((bf16[128,64,128]{2,1,0:T(8,128)(2,1)S(1)}, bf16[128,64,128]{2,1,0:T(8,128)(2,1)}, u32[]{:S(2)}) %copy-start) | copy-done | bytes 2097176
  21.0 0.0 copy-start.3
  21.0 0.9 copy-done.3
  21.9 21.2 %advance.1 = (bf16[16,128,256]{2,1,0:T(8,128)(2,1)S(1)}, bf16[17,128,256]{2,1,0:T(8,128)(2,1)S(1)}, bf16[128,4096]{1,0:T(8,128)(2,1)S(1)}) custom-call(s32[1]{0:T(128)} %bitcast.core.refs_0_, s32[1,128]{1,0:T(1,128)S(1)} %copy-done.6, s32[1,128]{1,0:T(1,128)S(1)} %copy-done.7, bf16[128,64,128]{2,1,0:T(8,128)(2,1)S(1)} %copy-done, ...), custom_call_target="tpu_custom_call" | custom-call | tf_op jit(solution)/shard_map/advance/pallas_call | solution.py:183
  43.2 0.0 copy-start.1
  43.2 1.0 %copy-done.1 = bf16[128,4096]{1,0:T(8,128)(2,1)} copy-done((bf16[128,4096]{1,0:T(8,128)(2,1)}, bf16[128,4096]{1,0:T(8,128)(2,1)S(1)}, u32[]{:S(2)}) %copy-start.1) | copy-done | bytes 1048600
  44.2 2.8 %collective-permute-start = (bf16[16,128,256]{2,1,0:T(8,128)(2,1)S(1)}, bf16[16,128,256]{2,1,0:T(8,128)(2,1)}, u32[]{:S(2)}, u32[]{:S(2)}) collective-permute-start(bf16[16,128,256]{2,1,0:T(8,128)(2,1)S(1)} %get-tuple-element.15), channel_id=1, source_target_pairs={{0,4},{4,0},{1,5},{5,1},{2,6},{6,2},{3,7},{7,3},{8,12},{12,8},{9,1... | collective-permute-start | bytes 3145736 | tf_op jit(solution)/shard_map/ppermute | solution.py:196
  47.0 2.4 %collective-permute-done.refs_4_ = bf16[16,128,256]{2,1,0:T(8,128)(2,1)} collective-permute-done((bf16[16,128,256]{2,1,0:T(8,128)(2,1)S(1)}, bf16[16,128,256]{2,1,0:T(8,128)(2,1)}, u32[]{:S(2)}, u32[]{:S(2)}) %collective-permute-start) | collective-permute-done | bytes 1048608 | tf_op jit(solution)/shard_map/ppermute | solution.py:196
  49.4 17.2 %all-to-all-done = bf16[64,128,128]{2,1,0:T(8,128)(2,1)S(1)} async-done(((bf16[64,128,128]{2,1,0:T(8,128)(2,1)}), bf16[64,128,128]{2,1,0:T(8,128)(2,1)S(1)}, u32[]{:S(2)}, u32[]{:S(2)}) %all-to-all-start) | async-done | bytes 2097184 | tf_op jit(solution)/shard_map/all_to_all | solution.py:170
  66.6 2.6 %amplitudes.1 = f32[64,128]{1,0:T(8,128)S(1)} custom-call(s32[1]{0:T(128)} %bitcast.core.refs_0_, bf16[17,128,256]{2,1,0:T(8,128)(2,1)S(1)} %get-tuple-element.14.refs_1_, bf16[64,2,64,128]{3,2,1,0:T(8,128)(2,1)S(1)} %bitcast.17, s32[1,4096]{1,0:T(1,128)S(1)} %reshape.40.owners.refs_3_, bf16[16,128,256]{2,1,0:T(8,128)(2,1)} %collective-permute-done.refs_4_, ...), custom_call_target="tpu_custom_call" | custom-call | tf_op jit(solution)/shard_map/amplitudes/pallas_call | solution.py:199
  69.2 10.9 %all_to_all.21.arrived = f32[8,8,128]{2,1,0:T(8,128)S(1)} all-to-all(f32[8,8,128]{2,1,0:T(8,128)S(1)} %bitcast.18), channel_id=1, replica_groups={{6,7,4,5,2,3,0,1},{14,15,12,13,10,11,8,9},{22,23,20,21,18,19,16,17},{30..., dimensions={0} | all-to-all | bytes 65536 | tf_op jit(solution)/shard_map/all_to_all | solution.py:225
  80.1 0.6 fold.1
  80.7 14.3 %all_to_all.22 = f32[64,1,128]{2,1,0:T(1,128)S(1)} all-to-all(f32[64,1,128]{2,1,0:T(1,128)} %bitcast.23), channel_id=1, replica_groups={{288,296,304,312,256,264,272,280,352,360,368,376,320,328,336,344,416,42..., dimensions={0} | all-to-all | bytes 65536 | tf_op jit(solution)/shard_map/all_to_all | solution.py:245
  95.0 0.7 finish.1
  (1 shorter events, 0.0 us)
Async XLA Ops:
  0.0 17.3 %copy-start.8 = (s32[4096]{0:T(1024)S(1)}, s32[4096]{0:T(1024)}, u32[]{:S(2)}) copy-start(s32[4096]{0:T(1024)} %param.17) | copy-start | bytes 49156
  0.0 66.6 %all-to-all-start = ((bf16[64,128,128]{2,1,0:T(8,128)(2,1)}), bf16[64,128,128]{2,1,0:T(8,128)(2,1)S(1)}, u32[]{:S(2)}, u32[]{:S(2)}) async-start(bf16[64,128,128]{2,1,0:T(8,128)(2,1)} %bitcast.20), calls=%async_computation | async-start | bytes 4194304 | tf_op jit(solution)/shard_map/all_to_all | solution.py:170
  17.3 2.1 %copy-start.2 = (bf16[128,8,128]{2,1,0:T(8,128)(2,1)S(1)}, bf16[128,8,128]{2,1,0:T(8,128)(2,1)}, u32[]{:S(2)}) copy-start(bf16[128,8,128]{2,1,0:T(8,128)(2,1)} %selectors.1) | copy-start | bytes 786436
  17.3 2.1 %copy-start.4 = (bf16[64,128]{1,0:T(8,128)(2,1)S(1)}, bf16[64,128]{1,0:T(8,128)(2,1)}, u32[]{:S(2)}) copy-start(bf16[64,128]{1,0:T(8,128)(2,1)} %left.1) | copy-start | bytes 49156
  17.3 2.1 %copy-start.5 = (bf16[64,128]{1,0:T(8,128)(2,1)S(1)}, bf16[64,128]{1,0:T(8,128)(2,1)}, u32[]{:S(2)}) copy-start(bf16[64,128]{1,0:T(8,128)(2,1)} %right.1) | copy-start | bytes 49156
  17.3 2.1 %copy-start.6 = (s32[1,128]{1,0:T(1,128)S(1)}, s32[1,128]{1,0:T(1,128)}, u32[]{:S(2)}) copy-start(s32[1,128]{1,0:T(1,128)} %levels.1) | copy-start | bytes 1540
  17.3 2.1 %copy-start.7 = (s32[1,128]{1,0:T(1,128)S(1)}, s32[1,128]{1,0:T(1,128)}, u32[]{:S(2)}) copy-start(s32[1,128]{1,0:T(1,128)} %sending.1) | copy-start | bytes 1540
  19.4 1.6 %copy-start = (bf16[128,64,128]{2,1,0:T(8,128)(2,1)S(1)}, bf16[128,64,128]{2,1,0:T(8,128)(2,1)}, u32[]{:S(2)}) copy-start(bf16[128,64,128]{2,1,0:T(8,128)(2,1)} %blocks.1) | copy-start | bytes 6291460
  21.0 0.9 copy-start.3
  43.2 1.0 %copy-start.1 = (bf16[128,4096]{1,0:T(8,128)(2,1)}, bf16[128,4096]{1,0:T(8,128)(2,1)S(1)}, u32[]{:S(2)}) copy-start(bf16[128,4096]{1,0:T(8,128)(2,1)S(1)} %get-tuple-element.16.refs_5_) | copy-start | bytes 3145732
  44.2 5.2 %collective-permute-start = (bf16[16,128,256]{2,1,0:T(8,128)(2,1)S(1)}, bf16[16,128,256]{2,1,0:T(8,128)(2,1)}, u32[]{:S(2)}, u32[]{:S(2)}) collective-permute-start(bf16[16,128,256]{2,1,0:T(8,128)(2,1)S(1)} %get-tuple-element.15), channel_id=1, source_target_pairs={{0,4},{4,0},{1,5},{5,1},{2,6},{6,2},{3,7},{7,3},{8,12},{12,8},{9,1... | collective-permute-start | bytes 3145736 | tf_op jit(solution)/shard_map/ppermute | solution.py:196
